TPU v7x, 256 devices: a whole 4x4x8 slice. The times are simulated.
256 devices in a mesh: slab: 32 (over y, z_lo, core), sub: 8 (over x, z_hi).
Axes of the slice: x: 4, y: 4, z: 8 (z_hi: 2, z_lo: 4; z = z_hi * 4 + z_lo), core: 2. Of those that a mesh axis runs over, the one named last changes fastest.
Arguments:
- rhs_interior: float32 [32, 32, 2, 256, 128], P('slab', 'sub'), may hold values from -6 to 6
- rhs_separator: float32 [32, 2, 512, 128], P('slab'), may hold values from -6 to 6
- inverse_blocks: float32 [32, 32, 2, 256, 256], P('slab', 'sub'), may hold values from -0.375 to 0.375
- coupling: float32 [32, 32, 2, 512, 256], P('slab', 'sub'), may hold values from -0.0625 to 0.0625
- separator_rows: int32 [32, 32, 512], P('slab', 'sub'), may hold values from 0 to 511, each once within a row
- separator_inverse: float32 [32, 2, 512, 512], P('slab'), may hold values from -1.1 to 1.1
- transfer: float32 [32, 2, 512, 512], P('slab'), may hold values from -1.1 to 1.1
Outputs:
- interior_solution: float32 [32, 32, 2, 256, 128], P('slab', 'sub')
- separator_solution: float32 [32, 2, 512, 128], P('slab')
Inputs may be any that keep to these rules, and one draw needn't show every extreme that they name: Each block's separator_rows lists every separator row 0 to 511 exactly once.
All inputs are finite; a program needn't handle non-finite values.
Results may differ from a plain program's by a relative error of at most 0.0003.
Values sent between devices are 32-bit elements; how exact they have to be, the bound alone decides.
A program may use at most 128 MiB of HBM per device.

v0:
```python
import jax
import jax.numpy as jnp
from jax import lax
from jax.sharding import PartitionSpec as P

HIGH = lax.Precision.HIGHEST


def from_behind(value, axis, steps):
    count = lax.axis_size(axis)
    first, last = (max(0, -steps), min(count, count - steps))
    return lax.ppermute(value, axis, [(source, source + steps) for source in range(first, last)])


def multiply(left, right):
    return jnp.matmul(left, right, precision=HIGH)


def complex_product(left, right):
    real_part = multiply(left[..., 0, :, :], right[..., 0, :, :]) - multiply(
        left[..., 1, :, :], right[..., 1, :, :]
    )
    imag_part = multiply(left[..., 0, :, :], right[..., 1, :, :]) + multiply(
        left[..., 1, :, :], right[..., 0, :, :]
    )
    return jnp.stack([real_part, imag_part], axis=-3)


def flipped(matrix):
    return jnp.swapaxes(matrix, -1, -2)


def body(
    rhs_interior,
    rhs_separator,
    inverse_blocks,
    coupling,
    separator_rows,
    separator_inverse,
    transfer,
):
    loads = rhs_interior[0]
    lower = inverse_blocks[0]
    rows = separator_rows[0]
    count = rows.shape[-1]
    spread = (rows[:, None, :] == jnp.arange(count)[None, :, None]).astype(jnp.float32)
    placed = jnp.einsum("bpr,bcrm->bcpm", spread, coupling[0], precision=HIGH)
    eliminated = complex_product(lower, loads)
    partial_load = jnp.sum(complex_product(placed, eliminated), axis=0)
    separator_load = lax.psum(partial_load, "sub")
    local = complex_product(separator_inverse[0], rhs_separator[0] - separator_load)
    mapping = transfer[0]
    backward_map = flipped(mapping)
    length = lax.axis_size("slab")
    position = lax.axis_index("slab")

    def forward_turn(step, state):
        trace_now, incoming = state
        trace_now = lax.cond(
            step == position, lambda: local - complex_product(mapping, incoming), lambda: trace_now
        )
        incoming = from_behind(trace_now, "slab", 1)
        return (trace_now, incoming)

    empty = jnp.zeros_like(local)
    traces, unused = lax.fori_loop(0, length, forward_turn, (empty, empty))

    def backward_turn(step, state):
        settled_now, exiting_trace, incoming = state

        def settle():
            value = traces - incoming
            return (value, complex_product(backward_map, value))

        settled_now, exiting_trace = lax.cond(
            step == length - 1 - position, settle, lambda: (settled_now, exiting_trace)
        )
        incoming = from_behind(exiting_trace, "slab", -1)
        return (settled_now, exiting_trace, incoming)

    finished_slabs, unused_out, unused_in = lax.fori_loop(
        0, length, backward_turn, (empty, empty, empty)
    )
    interior = complex_product(
        flipped(lower), eliminated - complex_product(flipped(placed), finished_slabs[None])
    )
    return (interior[None], finished_slabs[None])


def solution(mesh):
    in_specs = (
        P("slab", "sub", None, None, None),
        P("slab", None, None, None),
        P("slab", "sub", None, None, None),
        P("slab", "sub", None, None, None),
        P("slab", "sub", None),
        P("slab", None, None, None),
        P("slab", None, None, None),
    )
    out_specs = (P("slab", "sub", None, None, None), P("slab", None, None, None))
    return jax.shard_map(body, mesh=mesh, in_specs=in_specs, out_specs=out_specs, check_vma=False)
```

profile of v0, /device:TPU:1, one launch (start us, length us, event | category | flops | bytes accessed | tf_op | source)
XLA Modules:
  0.0 1166.5 jit_solution(15117272101623275622)
XLA Ops:
  29.5 107.2 %all-reduce.2.cloned.1.call-done = f32[2,512,128]{2,1,0:T(8,128)} async-done(((f32[2,512,128]{2,1,0:T(8,128)}), f32[2,512,128]{2,1,0:T(8,128)}) %all-reduce.2.cloned.1.call-update) | async-done | bytes 524304 | tf_op jit(solution)/shard_map/psum | solution.py:50
  145.5 396.4 %while.37 = (s32[]{:T(128)}, f32[2,512,128]{2,1,0:T(8,128)}, f32[2,512,128]{2,1,0:T(8,128)S(1)}, s32[]{:T(128)}, f32[2,512,512]{2,1,0:T(8,128)S(1)}, /*index=5*/f32[2,512,128]{2,1,0:T(8,128)S(1)}, s32[]{:T(128)}) while((s32[]{:T(128)}, f32[2,512,128]{2,1,0:T(8,128)}, f32[2,512,128]{2,1,0:T(8,128)S(1)}, s32[]{:T(128)}, ...), condition=%wide.region_5.0_spmd, body=%wide.region_2.0_spmd.sunk | while | flops 1611005952 | bytes 10485923 | solution.py:66
  145.5 9.0 collective-permute-start
  154.5 6.4 collective-permute-done
  167.7 6.4 collective-permute-done
  174.1 9.1 collective-permute-start
  183.2 6.4 collective-permute-done
  193.9 6.4 collective-permute-done
  204.6 6.4 collective-permute-done
  215.3 6.4 collective-permute-done
  340.9 7.0 collective-permute-start
  354.3 7.0 collective-permute-start
  367.7 7.0 collective-permute-start
  381.1 7.0 collective-permute-start
  394.5 7.0 collective-permute-start
  401.5 6.4 collective-permute-done
  407.9 7.0 collective-permute-start
  414.9 6.4 collective-permute-done
  421.3 7.0 collective-permute-start
  428.3 6.4 collective-permute-done
  434.7 7.0 collective-permute-start
  441.7 6.4 collective-permute-done
  448.1 7.0 collective-permute-start
  461.5 7.0 collective-permute-start
  474.9 7.0 collective-permute-start
  488.3 7.0 collective-permute-start
  501.7 7.0 collective-permute-start
  515.1 7.0 collective-permute-start
  522.1 6.4 collective-permute-done
  528.5 7.0 collective-permute-start
  535.5 6.4 collective-permute-done
  542.8 589.7 %while.38 = (s32[]{:T(128)}, f32[2,512,128]{2,1,0:T(8,128)}, f32[2,512,128]{1,2,0:T(8,128)S(1)}, f32[2,512,128]{1,2,0:T(8,128)S(1)}, s32[]{:T(128)}, /*index=5*/...) while((s32[]{:T(128)}, f32[2,512,128]{2,1,0:T(8,128)}, f32[2,512,128]{1,2,0:T(8,128)S(1)}, ...), condition=%wide.region_9.0_spmd, body=%wide.region_6.0_spmd.sunk | while | flops 1611005952 | bytes 20971752 | solution.py:81
  545.0 17.5 %collective-permute-done.1 = f32[2,512,128]{1,2,0:T(8,128)S(1)} collective-permute-done((f32[2,512,128]{1,2,0:T(8,128)S(1)}, f32[2,512,128]{1,2,0:T(8,128)S(1)}, u32[]{:S(2)}, u32[]{:S(2)}) %collective-permute-start.1) | collective-permute-done | bytes 524320 | tf_op jit(solution)/shard_map/while/body/eval_jaxpr/ppermute | solution.py:12
  564.5 12.9 %collective-permute-done.1 = f32[2,512,128]{1,2,0:T(8,128)S(1)} collective-permute-done((f32[2,512,128]{1,2,0:T(8,128)S(1)}, f32[2,512,128]{1,2,0:T(8,128)S(1)}, u32[]{:S(2)}, u32[]{:S(2)}) %collective-permute-start.1) | collective-permute-done | bytes 524320 | tf_op jit(solution)/shard_map/while/body/eval_jaxpr/ppermute | solution.py:12
  579.3 13.6 %collective-permute-done.1 = f32[2,512,128]{1,2,0:T(8,128)S(1)} collective-permute-done((f32[2,512,128]{1,2,0:T(8,128)S(1)}, f32[2,512,128]{1,2,0:T(8,128)S(1)}, u32[]{:S(2)}, u32[]{:S(2)}) %collective-permute-start.1) | collective-permute-done | bytes 524320 | tf_op jit(solution)/shard_map/while/body/eval_jaxpr/ppermute | solution.py:12
  594.8 9.7 collective-permute-done.1
  606.4 9.9 collective-permute-done.1
  618.3 11.2 collective-permute-done.1
  631.5 11.9 %collective-permute-done.1 = f32[2,512,128]{1,2,0:T(8,128)S(1)} collective-permute-done((f32[2,512,128]{1,2,0:T(8,128)S(1)}, f32[2,512,128]{1,2,0:T(8,128)S(1)}, u32[]{:S(2)}, u32[]{:S(2)}) %collective-permute-start.1) | collective-permute-done | bytes 524320 | tf_op jit(solution)/shard_map/while/body/eval_jaxpr/ppermute | solution.py:12
  645.3 11.3 collective-permute-done.1
  658.5 11.3 collective-permute-done.1
  671.7 11.3 collective-permute-done.1
  684.8 11.3 collective-permute-done.1
  698.0 11.3 collective-permute-done.1
  711.2 11.3 collective-permute-done.1
  724.4 11.3 collective-permute-done.1
  737.6 11.3 collective-permute-done.1
  750.8 11.3 collective-permute-done.1
  764.0 11.3 collective-permute-done.1
  777.1 11.3 collective-permute-done.1
  790.3 11.3 collective-permute-done.1
  803.5 11.3 collective-permute-done.1
  816.7 11.3 collective-permute-done.1
  829.9 11.3 collective-permute-done.1
  843.1 11.3 collective-permute-done.1
  856.3 11.3 collective-permute-done.1
  869.5 11.3 collective-permute-done.1
  882.6 11.3 collective-permute-done.1
  895.8 11.3 collective-permute-done.1
  909.0 11.3 collective-permute-done.1
  922.2 11.3 collective-permute-done.1
  935.4 165.1 %collective-permute-done.1 = f32[2,512,128]{1,2,0:T(8,128)S(1)} collective-permute-done((f32[2,512,128]{1,2,0:T(8,128)S(1)}, f32[2,512,128]{1,2,0:T(8,128)S(1)}, u32[]{:S(2)}, u32[]{:S(2)}) %collective-permute-start.1) | collective-permute-done | bytes 524320 | tf_op jit(solution)/shard_map/while/body/eval_jaxpr/ppermute | solution.py:12
  1100.5 11.1 conditional.5
  1113.5 8.6 collective-permute-done.1
  (211 shorter events, 340.2 us)
Async XLA Ops:
  7.2 129.5 %all-reduce.2.cloned.1.call-start = ((), (), s32[]{:S(2)}) async-start(), calls=%async_computation | async-start | bytes 1048576 | tf_op jit(solution)/shard_map/psum | solution.py:50
  145.5 15.4 %collective-permute-start = (f32[2,512,128]{2,1,0:T(8,128)}, f32[2,512,128]{2,1,0:T(8,128)S(1)}, u32[]{:S(2)}, u32[]{:S(2)}) collective-permute-start(f32[2,512,128]{2,1,0:T(8,128)} %get-tuple-element.502), channel_id=1, source_target_pairs={{0,8},{8,16},{16,24},{24,32},{32,40},{40,48},{48,56},{56,64},{64,7... | collective-permute-start | bytes 1572872 | tf_op jit(solution)/shard_map/while/body/eval_jaxpr/ppermute | solution.py:12
  174.1 15.5 %collective-permute-start = (f32[2,512,128]{2,1,0:T(8,128)}, f32[2,512,128]{2,1,0:T(8,128)S(1)}, u32[]{:S(2)}, u32[]{:S(2)}) collective-permute-start(f32[2,512,128]{2,1,0:T(8,128)} %get-tuple-element.502), channel_id=1, source_target_pairs={{0,8},{8,16},{16,24},{24,32},{32,40},{40,48},{48,56},{56,64},{64,7... | collective-permute-start | bytes 1572872 | tf_op jit(solution)/shard_map/while/body/eval_jaxpr/ppermute | solution.py:12
  189.6 10.7 collective-permute-start
  200.3 10.7 collective-permute-start
  211.0 10.7 collective-permute-start
  221.7 10.7 collective-permute-start
  232.4 10.7 collective-permute-start
  243.1 10.7 collective-permute-start
  253.8 10.7 collective-permute-start
  264.5 10.7 collective-permute-start
  275.2 10.7 collective-permute-start
  285.9 10.7 collective-permute-start
  296.6 10.7 collective-permute-start
  307.3 10.7 collective-permute-start
  318.0 10.7 collective-permute-start
  328.7 12.2 %collective-permute-start = (f32[2,512,128]{2,1,0:T(8,128)}, f32[2,512,128]{2,1,0:T(8,128)S(1)}, u32[]{:S(2)}, u32[]{:S(2)}) collective-permute-start(f32[2,512,128]{2,1,0:T(8,128)} %get-tuple-element.502), channel_id=1, source_target_pairs={{0,8},{8,16},{16,24},{24,32},{32,40},{40,48},{48,56},{56,64},{64,7... | collective-permute-start | bytes 1572872 | tf_op jit(solution)/shard_map/while/body/eval_jaxpr/ppermute | solution.py:12
  340.9 13.4 %collective-permute-start = (f32[2,512,128]{2,1,0:T(8,128)}, f32[2,512,128]{2,1,0:T(8,128)S(1)}, u32[]{:S(2)}, u32[]{:S(2)}) collective-permute-start(f32[2,512,128]{2,1,0:T(8,128)} %get-tuple-element.502), channel_id=1, source_target_pairs={{0,8},{8,16},{16,24},{24,32},{32,40},{40,48},{48,56},{56,64},{64,7... | collective-permute-start | bytes 1572872 | tf_op jit(solution)/shard_map/while/body/eval_jaxpr/ppermute | solution.py:12
  354.3 13.4 %collective-permute-start = (f32[2,512,128]{2,1,0:T(8,128)}, f32[2,512,128]{2,1,0:T(8,128)S(1)}, u32[]{:S(2)}, u32[]{:S(2)}) collective-permute-start(f32[2,512,128]{2,1,0:T(8,128)} %get-tuple-element.502), channel_id=1, source_target_pairs={{0,8},{8,16},{16,24},{24,32},{32,40},{40,48},{48,56},{56,64},{64,7... | collective-permute-start | bytes 1572872 | tf_op jit(solution)/shard_map/while/body/eval_jaxpr/ppermute | solution.py:12
  367.7 13.4 %collective-permute-start = (f32[2,512,128]{2,1,0:T(8,128)}, f32[2,512,128]{2,1,0:T(8,128)S(1)}, u32[]{:S(2)}, u32[]{:S(2)}) collective-permute-start(f32[2,512,128]{2,1,0:T(8,128)} %get-tuple-element.502), channel_id=1, source_target_pairs={{0,8},{8,16},{16,24},{24,32},{32,40},{40,48},{48,56},{56,64},{64,7... | collective-permute-start | bytes 1572872 | tf_op jit(solution)/shard_map/while/body/eval_jaxpr/ppermute | solution.py:12
  381.1 13.4 %collective-permute-start = (f32[2,512,128]{2,1,0:T(8,128)}, f32[2,512,128]{2,1,0:T(8,128)S(1)}, u32[]{:S(2)}, u32[]{:S(2)}) collective-permute-start(f32[2,512,128]{2,1,0:T(8,128)} %get-tuple-element.502), channel_id=1, source_target_pairs={{0,8},{8,16},{16,24},{24,32},{32,40},{40,48},{48,56},{56,64},{64,7... | collective-permute-start | bytes 1572872 | tf_op jit(solution)/shard_map/while/body/eval_jaxpr/ppermute | solution.py:12
  394.5 13.4 %collective-permute-start = (f32[2,512,128]{2,1,0:T(8,128)}, f32[2,512,128]{2,1,0:T(8,128)S(1)}, u32[]{:S(2)}, u32[]{:S(2)}) collective-permute-start(f32[2,512,128]{2,1,0:T(8,128)} %get-tuple-element.502), channel_id=1, source_target_pairs={{0,8},{8,16},{16,24},{24,32},{32,40},{40,48},{48,56},{56,64},{64,7... | collective-permute-start | bytes 1572872 | tf_op jit(solution)/shard_map/while/body/eval_jaxpr/ppermute | solution.py:12
  407.9 13.4 %collective-permute-start = (f32[2,512,128]{2,1,0:T(8,128)}, f32[2,512,128]{2,1,0:T(8,128)S(1)}, u32[]{:S(2)}, u32[]{:S(2)}) collective-permute-start(f32[2,512,128]{2,1,0:T(8,128)} %get-tuple-element.502), channel_id=1, source_target_pairs={{0,8},{8,16},{16,24},{24,32},{32,40},{40,48},{48,56},{56,64},{64,7... | collective-permute-start | bytes 1572872 | tf_op jit(solution)/shard_map/while/body/eval_jaxpr/ppermute | solution.py:12
  421.3 13.4 %collective-permute-start = (f32[2,512,128]{2,1,0:T(8,128)}, f32[2,512,128]{2,1,0:T(8,128)S(1)}, u32[]{:S(2)}, u32[]{:S(2)}) collective-permute-start(f32[2,512,128]{2,1,0:T(8,128)} %get-tuple-element.502), channel_id=1, source_target_pairs={{0,8},{8,16},{16,24},{24,32},{32,40},{40,48},{48,56},{56,64},{64,7... | collective-permute-start | bytes 1572872 | tf_op jit(solution)/shard_map/while/body/eval_jaxpr/ppermute | solution.py:12
  434.7 13.4 %collective-permute-start = (f32[2,512,128]{2,1,0:T(8,128)}, f32[2,512,128]{2,1,0:T(8,128)S(1)}, u32[]{:S(2)}, u32[]{:S(2)}) collective-permute-start(f32[2,512,128]{2,1,0:T(8,128)} %get-tuple-element.502), channel_id=1, source_target_pairs={{0,8},{8,16},{16,24},{24,32},{32,40},{40,48},{48,56},{56,64},{64,7... | collective-permute-start | bytes 1572872 | tf_op jit(solution)/shard_map/while/body/eval_jaxpr/ppermute | solution.py:12
  448.1 13.4 %collective-permute-start = (f32[2,512,128]{2,1,0:T(8,128)}, f32[2,512,128]{2,1,0:T(8,128)S(1)}, u32[]{:S(2)}, u32[]{:S(2)}) collective-permute-start(f32[2,512,128]{2,1,0:T(8,128)} %get-tuple-element.502), channel_id=1, source_target_pairs={{0,8},{8,16},{16,24},{24,32},{32,40},{40,48},{48,56},{56,64},{64,7... | collective-permute-start | bytes 1572872 | tf_op jit(solution)/shard_map/while/body/eval_jaxpr/ppermute | solution.py:12
  461.5 13.4 %collective-permute-start = (f32[2,512,128]{2,1,0:T(8,128)}, f32[2,512,128]{2,1,0:T(8,128)S(1)}, u32[]{:S(2)}, u32[]{:S(2)}) collective-permute-start(f32[2,512,128]{2,1,0:T(8,128)} %get-tuple-element.502), channel_id=1, source_target_pairs={{0,8},{8,16},{16,24},{24,32},{32,40},{40,48},{48,56},{56,64},{64,7... | collective-permute-start | bytes 1572872 | tf_op jit(solution)/shard_map/while/body/eval_jaxpr/ppermute | solution.py:12
  474.9 13.4 %collective-permute-start = (f32[2,512,128]{2,1,0:T(8,128)}, f32[2,512,128]{2,1,0:T(8,128)S(1)}, u32[]{:S(2)}, u32[]{:S(2)}) collective-permute-start(f32[2,512,128]{2,1,0:T(8,128)} %get-tuple-element.502), channel_id=1, source_target_pairs={{0,8},{8,16},{16,24},{24,32},{32,40},{40,48},{48,56},{56,64},{64,7... | collective-permute-start | bytes 1572872 | tf_op jit(solution)/shard_map/while/body/eval_jaxpr/ppermute | solution.py:12
  488.3 13.4 %collective-permute-start = (f32[2,512,128]{2,1,0:T(8,128)}, f32[2,512,128]{2,1,0:T(8,128)S(1)}, u32[]{:S(2)}, u32[]{:S(2)}) collective-permute-start(f32[2,512,128]{2,1,0:T(8,128)} %get-tuple-element.502), channel_id=1, source_target_pairs={{0,8},{8,16},{16,24},{24,32},{32,40},{40,48},{48,56},{56,64},{64,7... | collective-permute-start | bytes 1572872 | tf_op jit(solution)/shard_map/while/body/eval_jaxpr/ppermute | solution.py:12
  501.7 13.4 %collective-permute-start = (f32[2,512,128]{2,1,0:T(8,128)}, f32[2,512,128]{2,1,0:T(8,128)S(1)}, u32[]{:S(2)}, u32[]{:S(2)}) collective-permute-start(f32[2,512,128]{2,1,0:T(8,128)} %get-tuple-element.502), channel_id=1, source_target_pairs={{0,8},{8,16},{16,24},{24,32},{32,40},{40,48},{48,56},{56,64},{64,7... | collective-permute-start | bytes 1572872 | tf_op jit(solution)/shard_map/while/body/eval_jaxpr/ppermute | solution.py:12
  515.1 13.4 %collective-permute-start = (f32[2,512,128]{2,1,0:T(8,128)}, f32[2,512,128]{2,1,0:T(8,128)S(1)}, u32[]{:S(2)}, u32[]{:S(2)}) collective-permute-start(f32[2,512,128]{2,1,0:T(8,128)} %get-tuple-element.502), channel_id=1, source_target_pairs={{0,8},{8,16},{16,24},{24,32},{32,40},{40,48},{48,56},{56,64},{64,7... | collective-permute-start | bytes 1572872 | tf_op jit(solution)/shard_map/while/body/eval_jaxpr/ppermute | solution.py:12
  528.5 13.4 %collective-permute-start = (f32[2,512,128]{2,1,0:T(8,128)}, f32[2,512,128]{2,1,0:T(8,128)S(1)}, u32[]{:S(2)}, u32[]{:S(2)}) collective-permute-start(f32[2,512,128]{2,1,0:T(8,128)} %get-tuple-element.502), channel_id=1, source_target_pairs={{0,8},{8,16},{16,24},{24,32},{32,40},{40,48},{48,56},{56,64},{64,7... | collective-permute-start | bytes 1572872 | tf_op jit(solution)/shard_map/while/body/eval_jaxpr/ppermute | solution.py:12
  543.1 19.5 %collective-permute-start.1 = (f32[2,512,128]{1,2,0:T(8,128)S(1)}, f32[2,512,128]{1,2,0:T(8,128)S(1)}, u32[]{:S(2)}, u32[]{:S(2)}) collective-permute-start(f32[2,512,128]{1,2,0:T(8,128)S(1)} %get-tuple-element.496), channel_id=1, source_target_pairs={{8,0},{16,8},{24,16},{32,24},{40,32},{48,40},{56,48},{64,56},{72,6... | collective-permute-start | bytes 1572872 | tf_op jit(solution)/shard_map/while/body/eval_jaxpr/ppermute | solution.py:12
  562.5 14.9 %collective-permute-start.1 = (f32[2,512,128]{1,2,0:T(8,128)S(1)}, f32[2,512,128]{1,2,0:T(8,128)S(1)}, u32[]{:S(2)}, u32[]{:S(2)}) collective-permute-start(f32[2,512,128]{1,2,0:T(8,128)S(1)} %get-tuple-element.496), channel_id=1, source_target_pairs={{8,0},{16,8},{24,16},{32,24},{40,32},{48,40},{56,48},{64,56},{72,6... | collective-permute-start | bytes 1572872 | tf_op jit(solution)/shard_map/while/body/eval_jaxpr/ppermute | solution.py:12
  577.4 15.5 %collective-permute-start.1 = (f32[2,512,128]{1,2,0:T(8,128)S(1)}, f32[2,512,128]{1,2,0:T(8,128)S(1)}, u32[]{:S(2)}, u32[]{:S(2)}) collective-permute-start(f32[2,512,128]{1,2,0:T(8,128)S(1)} %get-tuple-element.496), channel_id=1, source_target_pairs={{8,0},{16,8},{24,16},{32,24},{40,32},{48,40},{56,48},{64,56},{72,6... | collective-permute-start | bytes 1572872 | tf_op jit(solution)/shard_map/while/body/eval_jaxpr/ppermute | solution.py:12
  592.9 11.6 collective-permute-start.1
  604.5 11.9 %collective-permute-start.1 = (f32[2,512,128]{1,2,0:T(8,128)S(1)}, f32[2,512,128]{1,2,0:T(8,128)S(1)}, u32[]{:S(2)}, u32[]{:S(2)}) collective-permute-start(f32[2,512,128]{1,2,0:T(8,128)S(1)} %get-tuple-element.496), channel_id=1, source_target_pairs={{8,0},{16,8},{24,16},{32,24},{40,32},{48,40},{56,48},{64,56},{72,6... | collective-permute-start | bytes 1572872 | tf_op jit(solution)/shard_map/while/body/eval_jaxpr/ppermute | solution.py:12
  616.4 13.2 %collective-permute-start.1 = (f32[2,512,128]{1,2,0:T(8,128)S(1)}, f32[2,512,128]{1,2,0:T(8,128)S(1)}, u32[]{:S(2)}, u32[]{:S(2)}) collective-permute-start(f32[2,512,128]{1,2,0:T(8,128)S(1)} %get-tuple-element.496), channel_id=1, source_target_pairs={{8,0},{16,8},{24,16},{32,24},{40,32},{48,40},{56,48},{64,56},{72,6... | collective-permute-start | bytes 1572872 | tf_op jit(solution)/shard_map/while/body/eval_jaxpr/ppermute | solution.py:12
  629.5 13.8 %collective-permute-start.1 = (f32[2,512,128]{1,2,0:T(8,128)S(1)}, f32[2,512,128]{1,2,0:T(8,128)S(1)}, u32[]{:S(2)}, u32[]{:S(2)}) collective-permute-start(f32[2,512,128]{1,2,0:T(8,128)S(1)} %get-tuple-element.496), channel_id=1, source_target_pairs={{8,0},{16,8},{24,16},{32,24},{40,32},{48,40},{56,48},{64,56},{72,6... | collective-permute-start | bytes 1572872 | tf_op jit(solution)/shard_map/while/body/eval_jaxpr/ppermute | solution.py:12
  643.4 13.2 %collective-permute-start.1 = (f32[2,512,128]{1,2,0:T(8,128)S(1)}, f32[2,512,128]{1,2,0:T(8,128)S(1)}, u32[]{:S(2)}, u32[]{:S(2)}) collective-permute-start(f32[2,512,128]{1,2,0:T(8,128)S(1)} %get-tuple-element.496), channel_id=1, source_target_pairs={{8,0},{16,8},{24,16},{32,24},{40,32},{48,40},{56,48},{64,56},{72,6... | collective-permute-start | bytes 1572872 | tf_op jit(solution)/shard_map/while/body/eval_jaxpr/ppermute | solution.py:12
  656.6 13.2 %collective-permute-start.1 = (f32[2,512,128]{1,2,0:T(8,128)S(1)}, f32[2,512,128]{1,2,0:T(8,128)S(1)}, u32[]{:S(2)}, u32[]{:S(2)}) collective-permute-start(f32[2,512,128]{1,2,0:T(8,128)S(1)} %get-tuple-element.496), channel_id=1, source_target_pairs={{8,0},{16,8},{24,16},{32,24},{40,32},{48,40},{56,48},{64,56},{72,6... | collective-permute-start | bytes 1572872 | tf_op jit(solution)/shard_map/while/body/eval_jaxpr/ppermute | solution.py:12
  669.7 13.2 %collective-permute-start.1 = (f32[2,512,128]{1,2,0:T(8,128)S(1)}, f32[2,512,128]{1,2,0:T(8,128)S(1)}, u32[]{:S(2)}, u32[]{:S(2)}) collective-permute-start(f32[2,512,128]{1,2,0:T(8,128)S(1)} %get-tuple-element.496), channel_id=1, source_target_pairs={{8,0},{16,8},{24,16},{32,24},{40,32},{48,40},{56,48},{64,56},{72,6... | collective-permute-start | bytes 1572872 | tf_op jit(solution)/shard_map/while/body/eval_jaxpr/ppermute | solution.py:12
  682.9 13.2 %collective-permute-start.1 = (f32[2,512,128]{1,2,0:T(8,128)S(1)}, f32[2,512,128]{1,2,0:T(8,128)S(1)}, u32[]{:S(2)}, u32[]{:S(2)}) collective-permute-start(f32[2,512,128]{1,2,0:T(8,128)S(1)} %get-tuple-element.496), channel_id=1, source_target_pairs={{8,0},{16,8},{24,16},{32,24},{40,32},{48,40},{56,48},{64,56},{72,6... | collective-permute-start | bytes 1572872 | tf_op jit(solution)/shard_map/while/body/eval_jaxpr/ppermute | solution.py:12
  696.1 13.2 %collective-permute-start.1 = (f32[2,512,128]{1,2,0:T(8,128)S(1)}, f32[2,512,128]{1,2,0:T(8,128)S(1)}, u32[]{:S(2)}, u32[]{:S(2)}) collective-permute-start(f32[2,512,128]{1,2,0:T(8,128)S(1)} %get-tuple-element.496), channel_id=1, source_target_pairs={{8,0},{16,8},{24,16},{32,24},{40,32},{48,40},{56,48},{64,56},{72,6... | collective-permute-start | bytes 1572872 | tf_op jit(solution)/shard_map/while/body/eval_jaxpr/ppermute | solution.py:12
  709.3 13.2 %collective-permute-start.1 = (f32[2,512,128]{1,2,0:T(8,128)S(1)}, f32[2,512,128]{1,2,0:T(8,128)S(1)}, u32[]{:S(2)}, u32[]{:S(2)}) collective-permute-start(f32[2,512,128]{1,2,0:T(8,128)S(1)} %get-tuple-element.496), channel_id=1, source_target_pairs={{8,0},{16,8},{24,16},{32,24},{40,32},{48,40},{56,48},{64,56},{72,6... | collective-permute-start | bytes 1572872 | tf_op jit(solution)/shard_map/while/body/eval_jaxpr/ppermute | solution.py:12
  722.5 13.2 %collective-permute-start.1 = (f32[2,512,128]{1,2,0:T(8,128)S(1)}, f32[2,512,128]{1,2,0:T(8,128)S(1)}, u32[]{:S(2)}, u32[]{:S(2)}) collective-permute-start(f32[2,512,128]{1,2,0:T(8,128)S(1)} %get-tuple-element.496), channel_id=1, source_target_pairs={{8,0},{16,8},{24,16},{32,24},{40,32},{48,40},{56,48},{64,56},{72,6... | collective-permute-start | bytes 1572872 | tf_op jit(solution)/shard_map/while/body/eval_jaxpr/ppermute | solution.py:12
  735.7 13.2 %collective-permute-start.1 = (f32[2,512,128]{1,2,0:T(8,128)S(1)}, f32[2,512,128]{1,2,0:T(8,128)S(1)}, u32[]{:S(2)}, u32[]{:S(2)}) collective-permute-start(f32[2,512,128]{1,2,0:T(8,128)S(1)} %get-tuple-element.496), channel_id=1, source_target_pairs={{8,0},{16,8},{24,16},{32,24},{40,32},{48,40},{56,48},{64,56},{72,6... | collective-permute-start | bytes 1572872 | tf_op jit(solution)/shard_map/while/body/eval_jaxpr/ppermute | solution.py:12
  748.9 13.2 %collective-permute-start.1 = (f32[2,512,128]{1,2,0:T(8,128)S(1)}, f32[2,512,128]{1,2,0:T(8,128)S(1)}, u32[]{:S(2)}, u32[]{:S(2)}) collective-permute-start(f32[2,512,128]{1,2,0:T(8,128)S(1)} %get-tuple-element.496), channel_id=1, source_target_pairs={{8,0},{16,8},{24,16},{32,24},{40,32},{48,40},{56,48},{64,56},{72,6... | collective-permute-start | bytes 1572872 | tf_op jit(solution)/shard_map/while/body/eval_jaxpr/ppermute | solution.py:12
  762.0 13.2 %collective-permute-start.1 = (f32[2,512,128]{1,2,0:T(8,128)S(1)}, f32[2,512,128]{1,2,0:T(8,128)S(1)}, u32[]{:S(2)}, u32[]{:S(2)}) collective-permute-start(f32[2,512,128]{1,2,0:T(8,128)S(1)} %get-tuple-element.496), channel_id=1, source_target_pairs={{8,0},{16,8},{24,16},{32,24},{40,32},{48,40},{56,48},{64,56},{72,6... | collective-permute-start | bytes 1572872 | tf_op jit(solution)/shard_map/while/body/eval_jaxpr/ppermute | solution.py:12
  775.2 13.2 %collective-permute-start.1 = (f32[2,512,128]{1,2,0:T(8,128)S(1)}, f32[2,512,128]{1,2,0:T(8,128)S(1)}, u32[]{:S(2)}, u32[]{:S(2)}) collective-permute-start(f32[2,512,128]{1,2,0:T(8,128)S(1)} %get-tuple-element.496), channel_id=1, source_target_pairs={{8,0},{16,8},{24,16},{32,24},{40,32},{48,40},{56,48},{64,56},{72,6... | collective-permute-start | bytes 1572872 | tf_op jit(solution)/shard_map/while/body/eval_jaxpr/ppermute | solution.py:12
  788.4 13.2 %collective-permute-start.1 = (f32[2,512,128]{1,2,0:T(8,128)S(1)}, f32[2,512,128]{1,2,0:T(8,128)S(1)}, u32[]{:S(2)}, u32[]{:S(2)}) collective-permute-start(f32[2,512,128]{1,2,0:T(8,128)S(1)} %get-tuple-element.496), channel_id=1, source_target_pairs={{8,0},{16,8},{24,16},{32,24},{40,32},{48,40},{56,48},{64,56},{72,6... | collective-permute-start | bytes 1572872 | tf_op jit(solution)/shard_map/while/body/eval_jaxpr/ppermute | solution.py:12
  801.6 13.2 %collective-permute-start.1 = (f32[2,512,128]{1,2,0:T(8,128)S(1)}, f32[2,512,128]{1,2,0:T(8,128)S(1)}, u32[]{:S(2)}, u32[]{:S(2)}) collective-permute-start(f32[2,512,128]{1,2,0:T(8,128)S(1)} %get-tuple-element.496), channel_id=1, source_target_pairs={{8,0},{16,8},{24,16},{32,24},{40,32},{48,40},{56,48},{64,56},{72,6... | collective-permute-start | bytes 1572872 | tf_op jit(solution)/shard_map/while/body/eval_jaxpr/ppermute | solution.py:12
  814.8 13.2 %collective-permute-start.1 = (f32[2,512,128]{1,2,0:T(8,128)S(1)}, f32[2,512,128]{1,2,0:T(8,128)S(1)}, u32[]{:S(2)}, u32[]{:S(2)}) collective-permute-start(f32[2,512,128]{1,2,0:T(8,128)S(1)} %get-tuple-element.496), channel_id=1, source_target_pairs={{8,0},{16,8},{24,16},{32,24},{40,32},{48,40},{56,48},{64,56},{72,6... | collective-permute-start | bytes 1572872 | tf_op jit(solution)/shard_map/while/body/eval_jaxpr/ppermute | solution.py:12
  828.0 13.2 %collective-permute-start.1 = (f32[2,512,128]{1,2,0:T(8,128)S(1)}, f32[2,512,128]{1,2,0:T(8,128)S(1)}, u32[]{:S(2)}, u32[]{:S(2)}) collective-permute-start(f32[2,512,128]{1,2,0:T(8,128)S(1)} %get-tuple-element.496), channel_id=1, source_target_pairs={{8,0},{16,8},{24,16},{32,24},{40,32},{48,40},{56,48},{64,56},{72,6... | collective-permute-start | bytes 1572872 | tf_op jit(solution)/shard_map/while/body/eval_jaxpr/ppermute | solution.py:12
  841.2 13.2 %collective-permute-start.1 = (f32[2,512,128]{1,2,0:T(8,128)S(1)}, f32[2,512,128]{1,2,0:T(8,128)S(1)}, u32[]{:S(2)}, u32[]{:S(2)}) collective-permute-start(f32[2,512,128]{1,2,0:T(8,128)S(1)} %get-tuple-element.496), channel_id=1, source_target_pairs={{8,0},{16,8},{24,16},{32,24},{40,32},{48,40},{56,48},{64,56},{72,6... | collective-permute-start | bytes 1572872 | tf_op jit(solution)/shard_map/while/body/eval_jaxpr/ppermute | solution.py:12
  854.3 13.2 %collective-permute-start.1 = (f32[2,512,128]{1,2,0:T(8,128)S(1)}, f32[2,512,128]{1,2,0:T(8,128)S(1)}, u32[]{:S(2)}, u32[]{:S(2)}) collective-permute-start(f32[2,512,128]{1,2,0:T(8,128)S(1)} %get-tuple-element.496), channel_id=1, source_target_pairs={{8,0},{16,8},{24,16},{32,24},{40,32},{48,40},{56,48},{64,56},{72,6... | collective-permute-start | bytes 1572872 | tf_op jit(solution)/shard_map/while/body/eval_jaxpr/ppermute | solution.py:12
  867.5 13.2 %collective-permute-start.1 = (f32[2,512,128]{1,2,0:T(8,128)S(1)}, f32[2,512,128]{1,2,0:T(8,128)S(1)}, u32[]{:S(2)}, u32[]{:S(2)}) collective-permute-start(f32[2,512,128]{1,2,0:T(8,128)S(1)} %get-tuple-element.496), channel_id=1, source_target_pairs={{8,0},{16,8},{24,16},{32,24},{40,32},{48,40},{56,48},{64,56},{72,6... | collective-permute-start | bytes 1572872 | tf_op jit(solution)/shard_map/while/body/eval_jaxpr/ppermute | solution.py:12
  880.7 13.2 %collective-permute-start.1 = (f32[2,512,128]{1,2,0:T(8,128)S(1)}, f32[2,512,128]{1,2,0:T(8,128)S(1)}, u32[]{:S(2)}, u32[]{:S(2)}) collective-permute-start(f32[2,512,128]{1,2,0:T(8,128)S(1)} %get-tuple-element.496), channel_id=1, source_target_pairs={{8,0},{16,8},{24,16},{32,24},{40,32},{48,40},{56,48},{64,56},{72,6... | collective-permute-start | bytes 1572872 | tf_op jit(solution)/shard_map/while/body/eval_jaxpr/ppermute | solution.py:12
  893.9 13.2 %collective-permute-start.1 = (f32[2,512,128]{1,2,0:T(8,128)S(1)}, f32[2,512,128]{1,2,0:T(8,128)S(1)}, u32[]{:S(2)}, u32[]{:S(2)}) collective-permute-start(f32[2,512,128]{1,2,0:T(8,128)S(1)} %get-tuple-element.496), channel_id=1, source_target_pairs={{8,0},{16,8},{24,16},{32,24},{40,32},{48,40},{56,48},{64,56},{72,6... | collective-permute-start | bytes 1572872 | tf_op jit(solution)/shard_map/while/body/eval_jaxpr/ppermute | solution.py:12
  907.1 13.2 %collective-permute-start.1 = (f32[2,512,128]{1,2,0:T(8,128)S(1)}, f32[2,512,128]{1,2,0:T(8,128)S(1)}, u32[]{:S(2)}, u32[]{:S(2)}) collective-permute-start(f32[2,512,128]{1,2,0:T(8,128)S(1)} %get-tuple-element.496), channel_id=1, source_target_pairs={{8,0},{16,8},{24,16},{32,24},{40,32},{48,40},{56,48},{64,56},{72,6... | collective-permute-start | bytes 1572872 | tf_op jit(solution)/shard_map/while/body/eval_jaxpr/ppermute | solution.py:12
  920.3 13.2 %collective-permute-start.1 = (f32[2,512,128]{1,2,0:T(8,128)S(1)}, f32[2,512,128]{1,2,0:T(8,128)S(1)}, u32[]{:S(2)}, u32[]{:S(2)}) collective-permute-start(f32[2,512,128]{1,2,0:T(8,128)S(1)} %get-tuple-element.496), channel_id=1, source_target_pairs={{8,0},{16,8},{24,16},{32,24},{40,32},{48,40},{56,48},{64,56},{72,6... | collective-permute-start | bytes 1572872 | tf_op jit(solution)/shard_map/while/body/eval_jaxpr/ppermute | solution.py:12
  933.5 167.0 %collective-permute-start.1 = (f32[2,512,128]{1,2,0:T(8,128)S(1)}, f32[2,512,128]{1,2,0:T(8,128)S(1)}, u32[]{:S(2)}, u32[]{:S(2)}) collective-permute-start(f32[2,512,128]{1,2,0:T(8,128)S(1)} %get-tuple-element.496), channel_id=1, source_target_pairs={{8,0},{16,8},{24,16},{32,24},{40,32},{48,40},{56,48},{64,56},{72,6... | collective-permute-start | bytes 1572872 | tf_op jit(solution)/shard_map/while/body/eval_jaxpr/ppermute | solution.py:12
  1111.6 10.5 collective-permute-start.1
  1122.1 10.5 collective-permute-start.1
  (16 other events, 182.3 us)
Sparse Core Ops, SparseCore 0:
  26.8 109.8 all-reduce.1
where the time goes:
time: 1180 us; the launch traced here: 1170 us
  waiting for transfers between devices  825 us (70%)
  starting transfers between devices  251 us (21%)
  matrix products  59 us (5%)
  between operations  14.8 us (1%)
    ppermute x64, waiting for transfers between devices, from_behind(): lax.ppermute(value, axis, [(source, source + steps) for source in range(f...  718 us
    ppermute x64, starting transfers between devices, from_behind(): lax.ppermute(value, axis, [(source, source + steps) for source in range(f...  251 us
    psum x1, waiting for transfers between devices, body(): separator_load = lax.psum(partial_load, 'sub')  107 us
    dot_general x28, matrix products, multiply(): return jnp.matmul(left, right, precision=HIGH)  54.9 us
  transfers between devices with their start and end apart: 65, of which 65 were waited for; matrix products, arithmetic and copies ran while one was open for 0% of the time, Pallas kernels for 0%

commit v1 on v0

v1 whole, which is shorter than its diff:
```python
import functools

import jax
import jax.numpy as jnp
from jax import lax
from jax.experimental import pallas as pl
from jax.experimental.pallas import tpu as pltpu
from jax.sharding import PartitionSpec as P

MESH = pl.DeviceIdType.MESH
F32 = jnp.float32
BF16 = jnp.bfloat16
NN = (((1,), (0,)), ((), ()))
NT = (((1,), (1,)), ((), ()))


def halves(value):
    high = value.astype(BF16)
    return high, (value - high.astype(F32)).astype(BF16)


def dot(left, right, dims=NN):
    return lax.dot_general(left, right, dims, preferred_element_type=F32)


def dot3(left, right, dims=NN):
    return dot(left[0], right[0], dims) + (
        dot(left[0], right[1], dims) + dot(left[1], right[0], dims)
    )


def times(value, high, low, dims):
    n = value.shape[0] // 2
    value_high, value_low = halves(value)
    both = jnp.concatenate([value_high, value_low], axis=0)
    out = []
    for part in range(2):
        whole = dot(both, high[part], dims)
        out.append(whole[: 2 * n] + (whole[2 * n :] + dot(value_high, low[part], dims)))
    return jnp.concatenate([out[0][:n] - out[1][n:], out[0][n:] + out[1][:n]], axis=0)


def load_kernel(rows_ref, rhs_ref, inverse_ref, coupling_ref, separator_ref, load_ref, elim_ref, total):
    block = pl.program_id(0)
    rhs = halves(jnp.concatenate([rhs_ref[0], rhs_ref[1]], axis=1))
    shots = rhs_ref.shape[-1]

    def product(matrix, right):
        real = dot3(halves(matrix[0]), right)
        imag = dot3(halves(matrix[1]), right)
        return jnp.concatenate(
            [real[:, :shots] - imag[:, shots:], real[:, shots:] + imag[:, :shots]], axis=1
        )

    eliminated = product(inverse_ref, rhs)
    elim_ref[...] = eliminated.T
    weighted = halves(product(coupling_ref, halves(eliminated)))
    count = rows_ref.shape[-1]
    spread = (lax.broadcasted_iota(jnp.int32, (count, count), 0) == rows_ref[...]).astype(BF16)
    placed = dot(spread, weighted[0]) + dot(spread, weighted[1])

    @pl.when(block == 0)
    def _():
        total[...] = placed

    @pl.when(block > 0)
    def _():
        total[...] += placed

    @pl.when(block == pl.num_programs(0) - 1)
    def _():
        given = jnp.concatenate([separator_ref[0], separator_ref[1]], axis=1)
        first = lax.axis_index("sub") == 0
        rest = (jnp.where(first, given, jnp.zeros_like(given)) - total[...]).T
        groups = shots // 8
        rest = rest.reshape(2, groups, 8, count)
        load_ref[...] = jnp.stack([rest[0], rest[1]], axis=1).reshape(load_ref.shape)


def loads_of(rhs_interior, rhs_separator, inverse_blocks, coupling, rows):
    nb, _, m, shots = rhs_interior.shape
    count = coupling.shape[2]
    subs = 8
    return pl.pallas_call(
        load_kernel,
        grid=(nb,),
        out_shape=(
            jax.ShapeDtypeStruct((subs, 2 * shots // subs, count), F32),
            jax.ShapeDtypeStruct((nb, 2 * shots, m), F32),
        ),
        in_specs=[
            pl.BlockSpec((None, 1, count), lambda b: (b, 0, 0)),
            pl.BlockSpec((None, 2, m, shots), lambda b: (b, 0, 0, 0)),
            pl.BlockSpec((None, 2, m, m), lambda b: (b, 0, 0, 0)),
            pl.BlockSpec((None, 2, count, m), lambda b: (b, 0, 0, 0)),
            pl.BlockSpec((2, count, shots), lambda b: (0, 0, 0)),
        ],
        out_specs=(
            pl.BlockSpec((subs, 2 * shots // subs, count), lambda b: (0, 0, 0)),
            pl.BlockSpec((None, 2 * shots, m), lambda b: (b, 0, 0)),
        ),
        scratch_shapes=[pltpu.VMEM((count, 2 * shots), F32)],
        compiler_params=pltpu.CompilerParams(vmem_limit_bytes=40 << 20),
    )(rows[:, None, :], rhs_interior, inverse_blocks, coupling, rhs_separator)


(C_MATRIX, C_X, C_Z, C_SWAP, C_AHEAD, C_BACK, C_CHIP, C_FAR, C_SIDE) = (0, 1, 4, 5, 6, 7, 8, 9, 10)
COPIES = 13


def sweep_kernel(
    load_ref,
    inverse_hbm,
    transfer_hbm,
    out_ref,
    pair,
    pair_high,
    pair_low,
    inverse,
    inverse_high,
    inverse_low,
    merged_high,
    merged_low,
    from_x,
    mine,
    from_z,
    local,
    spare,
    ahead_in,
    ahead_out,
    back_in,
    back_out,
    found,
    gathered,
    send_sem,
    recv_sem,
    here_sem,
):
    slab, sub = lax.axis_index("slab"), lax.axis_index("sub")
    chip, core = slab // 2, slab % 2
    chips = lax.axis_size("slab") // 2
    row, along = chip // 4, chip % 4
    x, far = sub // 2, sub % 2
    side = (far + row) % 2
    group = x * 2 + side
    partner = (slab + 1 - 2 * core, sub)
    opposite = (slab, x * 2 + (far + 1) % 2)
    ahead = ((slab + 2) % (2 * chips), x * 2 + (far + along // 3) % 2)
    behind = ((slab + 2 * chips - 2) % (2 * chips), x * 2 + (far + (3 - along) // 3) % 2)
    beside = [(slab, ((x + d) % 4) * 2 + far) for d in (1, 2, 3)]
    not_first, not_last = chip > 0, chip < chips - 1

    def remote(index, source, target, device):
        return pltpu.make_async_remote_copy(
            src_ref=source,
            dst_ref=target,
            send_sem=send_sem.at[index],
            recv_sem=recv_sem.at[index],
            device_id=device,
            device_id_type=MESH,
        )

    own_matrix = pltpu.make_async_copy(transfer_hbm, pair.at[core], here_sem.at[0])
    own_inverse = pltpu.make_async_copy(inverse_hbm, inverse, here_sem.at[1])
    own_matrix.start()
    own_inverse.start()

    barrier = pltpu.get_barrier_semaphore()

    def greet(device):
        pl.semaphore_signal(barrier, inc=1, device_id=device, device_id_type=MESH)

    for device in [partner, opposite] + beside:
        greet(device)
    pl.when(not_last)(lambda: greet(ahead))
    pl.when(not_first)(lambda: greet(behind))
    pl.semaphore_wait(
        barrier, 5 + (chip + chips - 1) // chips + (2 * chips - 2 - chip) // chips
    )

    x_copies = []
    for d in (1, 2, 3):
        to = (x + d) % 4
        copy = remote(C_X + d - 1, load_ref.at[pl.ds(2 * to, 2)], from_x.at[d - 1], beside[d - 1])
        copy.start()
        x_copies.append(copy)
    matrix_copy = remote(C_MATRIX, transfer_hbm, pair.at[core], partner)
    matrix_copy.start()

    size = pair.shape[-1]
    own_inverse.wait()

    def split_inverse(step, carry):
        at = pl.ds(pl.multiple_of(step * 128, 128), 128)
        for part in range(2):
            inverse_high[part, at, :], inverse_low[part, at, :] = halves(inverse[part, at, :])
        return carry

    lax.fori_loop(0, size // 128, split_inverse, 0)
    own_matrix.wait()
    for copy in x_copies:
        copy.wait_recv()
    mine[...] = (load_ref[pl.ds(2 * x, 2)] + from_x[0]) + (from_x[1] + from_x[2])
    z_copy = remote(C_Z, mine.at[1 - side], from_z, opposite)
    z_copy.start()

    remote(C_MATRIX, transfer_hbm, pair.at[1 - core], partner).wait_recv()

    def split_pair(step, carry):
        at = pl.ds(pl.multiple_of(step * 128, 128), 128)
        for slot in range(2):
            for part in range(2):
                pair_high[slot, part, at, :], pair_low[slot, part, at, :] = halves(
                    pair[slot, part, at, :]
                )
        return carry

    lax.fori_loop(0, size // 128, split_pair, 0)
    first = (pair_high.at[0], pair_low.at[0])
    second = (pair_high.at[1], pair_low.at[1])

    def merge(step, carry):
        at = pl.ds(pl.multiple_of(step * 128, 128), 128)
        left_high = jnp.concatenate([second[0][0, at, :], second[0][1, at, :]], axis=0)
        left_low = jnp.concatenate([second[1][0, at, :], second[1][1, at, :]], axis=0)
        out = [
            dot3((left_high, left_low), (first[0][part], first[1][part])) for part in range(2)
        ]
        merged = (out[0][:128] - out[1][128:], out[0][128:] + out[1][:128])
        for part in range(2):
            merged_high[part, at, :], merged_low[part, at, :] = halves(merged[part])
        return carry

    lax.fori_loop(0, size // 128, merge, 0)

    z_copy.wait_recv()
    summed = (mine[side] + from_z[...]).reshape(2, 2, 8, size)
    summed = jnp.stack([summed[:, 0], summed[:, 1]], axis=0).reshape(32, size)
    solved = times(summed, inverse_high, inverse_low, NT).reshape(2, 2, 8, size)
    solved = jnp.stack([solved[:, 0], solved[:, 1]], axis=0).reshape(2, 16, size)
    spare[...] = solved
    local[core] = spare[core]
    swap = remote(C_SWAP, spare.at[1 - core], local.at[core], partner)
    swap.start()

    @pl.when(chip == 0)
    def _():
        ahead_in[...] = jnp.zeros_like(ahead_in)

    @pl.when(chip == chips - 1)
    def _():
        back_in[...] = jnp.zeros_like(back_in)

    remote(C_SWAP, spare.at[0], local.at[1 - core], partner).wait_recv()

    start = local[1] - times(local[0], second[0], second[1], NT)
    ahead_copy = remote(C_AHEAD, ahead_out, ahead_in, ahead)
    pl.when(not_first)(ahead_copy.wait_recv)
    incoming = ahead_in[...]
    trace_second = start + times(incoming, merged_high, merged_low, NT)
    ahead_out[...] = trace_second
    pl.when(not_last)(ahead_copy.start)
    trace_first = local[0] - times(incoming, first[0], first[1], NT)
    queued = times(
        trace_first - times(trace_second, second[0], second[1], NN), first[0], first[1], NN
    )

    back_copy = remote(C_BACK, back_out, back_in, behind)
    pl.when(not_last)(back_copy.wait_recv)
    carried = back_in[...]

    @pl.when(not_first)
    def _():
        back_out[...] = queued + times(carried, merged_high, merged_low, NN)
        back_copy.start()

    found[1] = trace_second - carried
    found[0] = trace_first - times(found[1], second[0], second[1], NN)

    gathered[group, core] = found[core]
    chip_copy = remote(C_CHIP, found.at[1 - core], gathered.at[group, core], partner)
    chip_copy.start()
    remote(C_CHIP, found.at[0], gathered.at[group, 1 - core], partner).wait_recv()
    far_copy = remote(C_FAR, gathered.at[group], gathered.at[group], opposite)
    far_copy.start()
    other = x * 2 + 1 - side
    remote(C_FAR, gathered.at[other], gathered.at[other], opposite).wait_recv()
    for d in (1, 2, 3):
        piece = gathered.at[pl.ds(2 * x, 2)]
        remote(C_SIDE + d - 1, piece, piece, beside[d - 1]).start()
    for d in (1, 2, 3):
        piece = gathered.at[pl.ds(2 * ((x + 4 - d) % 4), 2)]
        remote(C_SIDE + d - 1, piece, piece, beside[d - 1]).wait_recv()
    out_ref[...] = gathered[...]

    for copy in x_copies:
        copy.wait_send()
    for copy in (matrix_copy, z_copy, swap, chip_copy, far_copy):
        copy.wait_send()
    pl.when(not_last)(ahead_copy.wait_send)
    pl.when(not_first)(back_copy.wait_send)
    for d in (1, 2, 3):
        piece = gathered.at[pl.ds(2 * x, 2)]
        remote(C_SIDE + d - 1, piece, piece, beside[d - 1]).wait_send()


def sweeps_of(load, separator_inverse, transfer):
    size = transfer.shape[-1]
    vmem = pltpu.VMEM
    return pl.pallas_call(
        sweep_kernel,
        out_shape=jax.ShapeDtypeStruct((8, 2, 16, size), F32),
        in_specs=[
            pl.BlockSpec(memory_space=pltpu.VMEM),
            pl.BlockSpec(memory_space=pl.ANY),
            pl.BlockSpec(memory_space=pl.ANY),
        ],
        out_specs=pl.BlockSpec(memory_space=pltpu.VMEM),
        scratch_shapes=[
            vmem((2, 2, size, size), F32),
            vmem((2, 2, size, size), BF16),
            vmem((2, 2, size, size), BF16),
            vmem((2, size, size), F32),
            vmem((2, size, size), BF16),
            vmem((2, size, size), BF16),
            vmem((2, size, size), BF16),
            vmem((2, size, size), BF16),
            vmem((3, 2, 32, size), F32),
            vmem((2, 32, size), F32),
            vmem((32, size), F32),
            vmem((2, 16, size), F32),
            vmem((2, 16, size), F32),
            vmem((16, size), F32),
            vmem((16, size), F32),
            vmem((16, size), F32),
            vmem((16, size), F32),
            vmem((2, 16, size), F32),
            vmem((8, 2, 16, size), F32),
            pltpu.SemaphoreType.DMA((COPIES,)),
            pltpu.SemaphoreType.DMA((COPIES,)),
            pltpu.SemaphoreType.DMA((2,)),
        ],
        compiler_params=pltpu.CompilerParams(
            collective_id=0, has_side_effects=True, vmem_limit_bytes=48 << 20
        ),
    )(load, separator_inverse, transfer)


def interior_kernel(
    rows_ref, found_ref, elim_ref, inverse_ref, coupling_ref, interior_ref, separator_ref, high, low
):
    shots = interior_ref.shape[-1]
    count = rows_ref.shape[-1]

    @pl.when(pl.program_id(0) == 0)
    def _():
        found = found_ref[...].reshape(shots // 8, 2, 8, count)
        value = jnp.stack([found[:, 0], found[:, 1]], axis=0).reshape(2 * shots, count)
        high[...], low[...] = halves(value)
        turned = value.T
        separator_ref[0] = turned[:, :shots]
        separator_ref[1] = turned[:, shots:]

    def product(left, matrix):
        left = halves(left)
        real = dot3(left, halves(matrix[0]))
        imag = dot3(left, halves(matrix[1]))
        return jnp.concatenate(
            [real[:shots] - imag[shots:], real[shots:] + imag[:shots]], axis=0
        )

    spread = (lax.broadcasted_iota(jnp.int32, (count, count), 0) == rows_ref[...]).astype(BF16)
    picked = dot(high[...], spread) + dot(low[...], spread)
    rest = elim_ref[...] - product(picked, coupling_ref)
    turned = product(rest, inverse_ref).T
    interior_ref[0] = turned[:, :shots]
    interior_ref[1] = turned[:, shots:]


def interiors_of(found, eliminated, inverse_blocks, coupling, rows):
    nb, _, count, m = coupling.shape
    shots = eliminated.shape[1] // 2
    return pl.pallas_call(
        interior_kernel,
        grid=(nb,),
        out_shape=(
            jax.ShapeDtypeStruct((nb, 2, m, shots), F32),
            jax.ShapeDtypeStruct((2, count, shots), F32),
        ),
        in_specs=[
            pl.BlockSpec((None, 1, count), lambda b: (b, 0, 0)),
            pl.BlockSpec(found.shape, lambda b: (0, 0, 0, 0)),
            pl.BlockSpec((None, 2 * shots, m), lambda b: (b, 0, 0)),
            pl.BlockSpec((None, 2, m, m), lambda b: (b, 0, 0, 0)),
            pl.BlockSpec((None, 2, count, m), lambda b: (b, 0, 0, 0)),
        ],
        out_specs=(
            pl.BlockSpec((None, 2, m, shots), lambda b: (b, 0, 0, 0)),
            pl.BlockSpec((2, count, shots), lambda b: (0, 0, 0)),
        ),
        scratch_shapes=[
            pltpu.VMEM((2 * shots, count), BF16),
            pltpu.VMEM((2 * shots, count), BF16),
        ],
        compiler_params=pltpu.CompilerParams(vmem_limit_bytes=40 << 20),
    )(rows[:, None, :], found, eliminated, inverse_blocks, coupling)


def body(
    rhs_interior,
    rhs_separator,
    inverse_blocks,
    coupling,
    separator_rows,
    separator_inverse,
    transfer,
):
    rows = separator_rows[0]
    load, eliminated = loads_of(
        rhs_interior[0], rhs_separator[0], inverse_blocks[0], coupling[0], rows
    )
    found = sweeps_of(load, separator_inverse[0], transfer[0])
    interior, separator = interiors_of(found, eliminated, inverse_blocks[0], coupling[0], rows)
    return (interior[None], separator[None])


def solution(mesh):
    in_specs = (
        P("slab", "sub", None, None, None),
        P("slab", None, None, None),
        P("slab", "sub", None, None, None),
        P("slab", "sub", None, None, None),
        P("slab", "sub", None),
        P("slab", None, None, None),
        P("slab", None, None, None),
    )
    out_specs = (P("slab", "sub", None, None, None), P("slab", None, None, None))
    return jax.shard_map(body, mesh=mesh, in_specs=in_specs, out_specs=out_specs, check_vma=False)
```

time: 1180 us -> 175 us (0.15); the launches traced: 1170 us -> 175 us
  waiting for transfers between devices: 825 us -> 0 us
  starting transfers between devices: 251 us -> 0 us
  Pallas kernels: 0 us -> 167 us
  matrix products: 59 us -> 0 us
  between operations: 14.8 us -> 0.69 us
    ppermute x64 -> x0, waiting for transfers between devices: 718 us -> none  [from_behind(): lax.ppermute(value, axis, [(source, source + steps) for source in range(f...]
    ppermute x64 -> x0, starting transfers between devices: 251 us -> none  [from_behind(): lax.ppermute(value, axis, [(source, source + steps) for source in range(f...]
    pallas_call x0 -> x3, Pallas kernels: none -> 167 us  [the longest x1 150 us: sweeps_of(): pl.pallas_call(sweep_kernel, out_shape=jax.ShapeDtypeStruct((8, 2, 16, si...]
    psum x1 -> x0, waiting for transfers between devices: 107 us -> none  [body(): separator_load = lax.psum(partial_load, 'sub')]
    dot_general x29 -> x0, matrix products: 59 us -> none  [the longest x28 54.9 us: multiply(): return jnp.matmul(left, right, precision=HIGH)]
  transfers between devices with their start and end apart: 65 -> 0, of which waited for: 65 -> 0; matrix products, arithmetic and copies ran while one was open for 0% -> 0% of each run, Pallas kernels for 0% -> 0%
where the time goes in v1:
time: 175 us
  Pallas kernels  167 us (95%)
  local copies, waits for them, and re-layouts  6.76 us (4%)
    pallas_call x1, Pallas kernels, sweeps_of(): pl.pallas_call(sweep_kernel, out_shape=jax.ShapeDtypeStruct((8, 2, 16, si...  150 us
    pallas_call x1, Pallas kernels, interiors_of(): pl.pallas_call(interior_kernel, grid=(nb,), out_shape=(jax.ShapeDtypeStru...  9.18 us
    pallas_call x1, Pallas kernels, loads_of(): pl.pallas_call(load_kernel, grid=(nb,), out_shape=(jax.ShapeDtypeStruct((...  7.63 us
    unnamed x16, local copies, waits for them, and re-layouts  6.06 us

profile of v1, /device:TPU:1, one launch (start us, length us, event | category | flops | bytes accessed | tf_op | source)
XLA Modules:
  0.0 174.5 jit_solution(966084992857524897)
XLA Ops:
  0.6 0.7 broadcast_in_dim_squeeze.4.rows_ref
  1.3 0.0 copy-start
  1.3 2.2 %copy-done = f32[1,4,2,512,256]{4,3,2,1,0:T(8,128)S(1)} copy-done((f32[1,4,2,512,256]{4,3,2,1,0:T(8,128)S(1)}, f32[1,4,2,512,256]{4,3,2,1,0:T(8,128)}, u32[]{:S(2)}) %copy-start) | copy-done | bytes 4194328
  3.5 0.0 copy-start.2
  3.5 1.6 copy-done.2
  5.1 0.0 copy-start.6
  5.1 1.2 copy-done.6
  6.3 0.0 copy-start.7
  6.3 1.0 copy-done.7
  7.4 0.0 copy-start.4
  7.4 0.0 copy-start.5
  7.4 0.0 copy-start.3
  7.4 7.6 %shard_map.86 = (f32[8,32,512]{2,1,0:T(8,128)S(1)}, f32[4,256,256]{2,1,0:T(8,128)S(1)}) custom-call(s32[4,1,512]{2,1,0:T(1,128)S(1)} %broadcast_in_dim_squeeze.4.rows_ref, f32[4,2,256,128]{3,2,1,0:T(8,128)S(1)} %bitcast.14, f32[4,2,256,256]{3,2,1,0:T(8,128)S(1)} %bitcast.10, f32[4,2,512,256]{3,2,1,0:T(8,128)S(1)} %bitcast.8, f32[2,512,128]{2,1,0:T(8,128)S(1)} %bitcast.15), custom_call_target="tpu_custom_call" | custom-call | tf_op jit(solution)/shard_map/pallas_call | solution.py:84
  15.0 0.0 copy-done.4
  15.0 0.0 copy-done.5
  15.0 0.0 copy-start.1
  15.1 150.2 %shard_map.87.found_ref = f32[8,2,16,512]{3,2,1,0:T(8,128)S(1)} custom-call(f32[8,32,512]{2,1,0:T(8,128)S(1)} %get-tuple-element.6.load_ref, f32[2,512,512]{2,1,0:T(8,128)S(1)} %bitcast.12, f32[2,512,512]{2,1,0:T(8,128)S(1)} %bitcast.13), custom_call_target="tpu_custom_call" | custom-call | tf_op jit(solution)/shard_map/pallas_call | solution.py:310
  165.3 0.0 copy-done.3
  165.3 0.0 copy-done.1
  165.3 9.2 %shard_map.88 = (f32[4,2,256,128]{3,2,1,0:T(8,128)}, f32[2,512,128]{2,1,0:T(8,128)}) custom-call(s32[4,1,512]{2,1,0:T(1,128)S(1)} %broadcast_in_dim_squeeze.4.rows_ref, f32[8,2,16,512]{3,2,1,0:T(8,128)S(1)} %shard_map.87.found_ref, f32[4,256,256]{2,1,0:T(8,128)S(1)} %get-tuple-element.7.elim_ref, f32[4,2,256,256]{3,2,1,0:T(8,128)S(1)} %bitcast.11, ...), custom_call_target="tpu_custom_call" | custom-call | tf_op jit(solution)/shard_map/pallas_call | solution.py:383
Async XLA Ops:
  1.3 2.2 %copy-start = (f32[1,4,2,512,256]{4,3,2,1,0:T(8,128)S(1)}, f32[1,4,2,512,256]{4,3,2,1,0:T(8,128)}, u32[]{:S(2)}) copy-start(f32[1,4,2,512,256]{4,3,2,1,0:T(8,128)} %param.10) | copy-start | bytes 12582916
  3.5 1.6 copy-start.2
  5.1 1.2 copy-start.6
  6.3 1.0 copy-start.7
  7.4 7.6 %copy-start.4 = (f32[1,2,512,512]{3,2,1,0:T(8,128)S(1)}, f32[1,2,512,512]{3,2,1,0:T(8,128)}, u32[]{:S(2)}) copy-start(f32[1,2,512,512]{3,2,1,0:T(8,128)} %param.12) | copy-start | bytes 6291460
  7.4 7.7 %copy-start.5 = (f32[1,2,512,512]{3,2,1,0:T(8,128)S(1)}, f32[1,2,512,512]{3,2,1,0:T(8,128)}, u32[]{:S(2)}) copy-start(f32[1,2,512,512]{3,2,1,0:T(8,128)} %param.13) | copy-start | bytes 6291460
  7.4 157.9 %copy-start.3 = (f32[1,4,2,256,256]{4,3,2,1,0:T(8,128)S(1)}, f32[1,4,2,256,256]{4,3,2,1,0:T(8,128)}, u32[]{:S(2)}) copy-start(f32[1,4,2,256,256]{4,3,2,1,0:T(8,128)} %param.9) | copy-start | bytes 6291460
  15.0 150.3 %copy-start.1 = (f32[1,4,2,512,256]{4,3,2,1,0:T(8,128)S(1)}, f32[1,4,2,512,256]{4,3,2,1,0:T(8,128)}, u32[]{:S(2)}) copy-start(f32[1,4,2,512,256]{4,3,2,1,0:T(8,128)} %param.10) | copy-start | bytes 12582916

commit v2 on v0

v2 whole, which is shorter than its diff:
```python
import types

import jax
import jax.numpy as jnp
from jax import lax
from jax.experimental import pallas as pl
from jax.experimental.pallas import tpu as pltpu
from jax.sharding import PartitionSpec as P

MESH = pl.DeviceIdType.MESH
F32 = jnp.float32
BF16 = jnp.bfloat16
NN = (((1,), (0,)), ((), ()))
NT = (((1,), (1,)), ((), ()))
STRIP = 128


def halves(value):
    high = value.astype(BF16)
    return high, (value - high.astype(F32)).astype(BF16)


def dot(left, right, dims=NN):
    return lax.dot_general(left, right, dims, preferred_element_type=F32)


def dot3(left, right, dims=NN):
    return dot(left[0], right[0], dims) + (
        dot(left[0], right[1], dims) + dot(left[1], right[0], dims)
    )


def times(value, matrix, dims):
    high, low = matrix
    n = value.shape[0] // 2
    value_high, value_low = halves(value)
    both = jnp.concatenate([value_high, value_low], axis=0)
    out = []
    for part in range(2):
        whole = dot(both, high[part], dims)
        out.append(whole[: 2 * n] + (whole[2 * n :] + dot(value_high, low[part], dims)))
    return jnp.concatenate([out[0][:n] - out[1][n:], out[0][n:] + out[1][:n]], axis=0)


def kernel(names, *refs):
    r = types.SimpleNamespace(**dict(zip(names, refs)))
    slab, sub = lax.axis_index("slab"), lax.axis_index("sub")
    slabs = lax.axis_size("slab")
    core, role, duo = slab % 2, (slab // 2) % 2, slab // 4
    duos = slabs // 4
    x, far = sub // 2, sub % 2
    after, before = (2 * duos - 3 - duo) // (duos - 1), (duo + duos - 2) // (duos - 1)
    has_after, has_before = duo < duos - 1, duo > 0
    early, late = role == 0, role == 1
    blocks, _, size, m = r.coupling_hbm.shape
    shots = r.rhs_hbm.shape[-1]

    other_core, other_sub = slab + 1 - 2 * core, 2 * x + 1 - far
    partner = (other_core, sub)
    opposite = (slab, other_sub)
    across = (other_core, other_sub)
    mate = (slab + 2 - 4 * role, sub)
    beside = [(slab, ((x + d) % 4) * 2 + far) for d in (1, 2, 3)]
    next_late, next_early = ((slab + 4) % slabs, sub), ((slab + 2) % slabs, sub)
    last_early, last_late = ((slab + slabs - 4) % slabs, sub), ((slab + slabs - 2) % slabs, sub)

    count = [0]
    unsent = []

    def remote(index, source, target, device):
        return pltpu.make_async_remote_copy(
            src_ref=source,
            dst_ref=target,
            send_sem=r.send_sem.at[index],
            recv_sem=r.recv_sem.at[index],
            device_id=device,
            device_id_type=MESH,
        )

    def channel():
        count[0] += 1
        return count[0] - 1

    def send(index, source, target, device, when=None):
        copy = remote(index, source, target, device)
        if when is None:
            copy.start()
        unsent.append((copy, when))
        return copy

    def receive(index, target):
        remote(index, target, target, partner).wait_recv()

    def local_copies(b):
        return [
            pltpu.make_async_copy(r.inverse_hbm.at[b], r.inverse.at[b], r.block_sem.at[0, b]),
            pltpu.make_async_copy(r.rhs_hbm.at[b], r.rhs.at[b], r.block_sem.at[1, b]),
            pltpu.make_async_copy(r.coupling_hbm.at[b], r.coupling.at[b], r.block_sem.at[2, b]),
        ]

    own_transfer = pltpu.make_async_copy(r.transfer_hbm, r.pair.at[core], r.here_sem.at[0])
    own_given = pltpu.make_async_copy(r.separator_hbm, r.given, r.here_sem.at[1])
    own_schur = pltpu.make_async_copy(r.schur_hbm, r.schur, r.here_sem.at[2])
    own_transfer.start()

    barrier = pltpu.get_barrier_semaphore()

    def greet(device):
        pl.semaphore_signal(barrier, inc=1, device_id=device, device_id_type=MESH)

    for device in [partner, opposite, across, mate] + beside:
        greet(device)

    @pl.when(has_after)
    def _():
        greet(next_late)

        @pl.when(late)
        def _():
            greet(next_early)

    @pl.when(has_before)
    def _():
        greet(last_early)

        @pl.when(early)
        def _():
            greet(last_late)

    pl.semaphore_wait(barrier, 7 + after + before + role * after + (1 - role) * before)

    c_transfer = channel()
    send(c_transfer, r.transfer_hbm, r.pair.at[core], partner)
    for b in range(blocks):
        for copy in local_copies(b):
            copy.start()
    own_given.start()
    own_schur.start()

    own_transfer.wait()
    receive(c_transfer, r.pair.at[1 - core])

    def split_pair(step, carry):
        at = pl.ds(pl.multiple_of(step * STRIP, STRIP), STRIP)
        for slot in range(2):
            for part in range(2):
                r.pair_high[slot, part, at, :], r.pair_low[slot, part, at, :] = halves(
                    r.pair[slot, part, at, :]
                )
        return carry

    lax.fori_loop(0, size // STRIP, split_pair, 0)
    first = (r.pair_high.at[0], r.pair_low.at[0])
    second = (r.pair_high.at[1], r.pair_low.at[1])

    def merged_rows(left, at, right):
        rows_high = jnp.concatenate([left[0][0, at, :], left[0][1, at, :]], axis=0)
        rows_low = jnp.concatenate([left[1][0, at, :], left[1][1, at, :]], axis=0)
        out = [dot3((rows_high, rows_low), (right[0][part], right[1][part])) for part in range(2)]
        return out[0][:STRIP] - out[1][STRIP:], out[0][STRIP:] + out[1][:STRIP]

    half = size // 2

    def merge_two(step, carry):
        at = pl.ds(pl.multiple_of(core * half + step * STRIP, STRIP), STRIP)
        to = pl.ds(pl.multiple_of(step * STRIP, STRIP), STRIP)
        merged = merged_rows(second, at, first)
        for part in range(2):
            r.twos[role, core, part, to, :] = merged[part]
        return carry

    lax.fori_loop(0, half // STRIP, merge_two, 0)
    c_half, c_mate, c_pass = channel(), channel(), channel()
    send(c_mate, r.twos.at[role, core], r.twos.at[role, core], mate)
    send(c_half, r.twos.at[role, core], r.twos.at[role, core], partner)

    def combine(real, imag, axis):
        n = real.shape[axis] // 2
        if axis == 1:
            return jnp.concatenate(
                [real[:, :n] - imag[:, n:], real[:, n:] + imag[:, :n]], axis=1
            )
        return jnp.concatenate([real[:n] - imag[n:], real[n:] + imag[:n]], axis=0)

    r.total[...] = jnp.zeros_like(r.total)

    def load_of(b, carry):
        for copy in local_copies(b):
            copy.wait()
        for source, high, low in (
            (r.inverse, r.inverse_high, r.inverse_low),
            (r.coupling, r.coupling_high, r.coupling_low),
        ):
            for part in range(2):
                high[b, part], low[b, part] = halves(source[b, part])

        def product(high, low, right):
            right = halves(right)
            out = [dot3((high[b, part], low[b, part]), right) for part in range(2)]
            return combine(out[0], out[1], 1)

        eliminated = product(
            r.inverse_high, r.inverse_low, jnp.concatenate([r.rhs[b, 0], r.rhs[b, 1]], axis=1)
        )
        r.eliminated[b] = eliminated.T
        weighted = halves(product(r.coupling_high, r.coupling_low, eliminated))
        spread = (lax.broadcasted_iota(jnp.int32, (size, size), 0) == r.rows[b]).astype(BF16)
        r.spread[b] = spread
        r.total[...] += dot(spread, weighted[0]) + dot(spread, weighted[1])
        return carry

    lax.fori_loop(0, blocks, load_of, 0)
    own_given.wait()
    given = jnp.concatenate([r.given[0], r.given[1]], axis=1)
    rest = (jnp.where(sub == 0, given, jnp.zeros_like(given)) - r.total[...]).T
    rest = rest.reshape(2, shots // 8, 8, size)
    r.load[...] = jnp.stack([rest[0], rest[1]], axis=1).reshape(r.load.shape)

    c_x = [[channel() for d in range(3)] for which in range(2)]
    c_z = channel()
    for which in range(2):
        for d in (1, 2, 3):
            group = 2 * ((x + d) % 4) + (1 - far if which == 0 else far)
            send(
                c_x[which][d - 1], r.load.at[group], r.from_x.at[which, d - 1], beside[d - 1]
            )

    own_schur.wait()

    def split_schur(step, carry):
        at = pl.ds(pl.multiple_of(step * STRIP, STRIP), STRIP)
        for part in range(2):
            r.schur_high[part, :, at], r.schur_low[part, :, at] = halves(r.schur[part, at, :].T)
        return carry

    lax.fori_loop(0, size // STRIP, split_schur, 0)

    def side_sum(which, group):
        for d in range(3):
            receive(c_x[which][d], r.from_x.at[which, d])
        return (r.load[group] + r.from_x[which, 0]) + (r.from_x[which, 1] + r.from_x[which, 2])

    r.forward_sum[...] = side_sum(0, other_sub)
    send(c_z, r.forward_sum, r.from_z, opposite)
    own_sum = side_sum(1, sub)

    receive(c_half, r.twos.at[role, 1 - core])

    def split_two(which):
        def step_of(step, carry):
            piece, at = step // 2, pl.ds(pl.multiple_of((step % 2) * STRIP, STRIP), STRIP)
            to = pl.ds(pl.multiple_of(step * STRIP, STRIP), STRIP)
            for part in range(2):
                r.two_high[which, part, to, :], r.two_low[which, part, to, :] = halves(
                    r.twos[which, piece, part, at, :]
                )
            return carry

        lax.fori_loop(0, size // STRIP, step_of, 0)

    split_two(role)
    two_early = (r.two_high.at[0], r.two_low.at[0])
    two_late = (r.two_high.at[1], r.two_low.at[1])
    four = (r.four_high, r.four_low)

    receive(c_z, r.from_z)
    summed = (own_sum + r.from_z[...]).reshape(2, 2, 8, size)
    summed = jnp.stack([summed[:, 0], summed[:, 1]], axis=0).reshape(32, size)
    solved = times(summed, (r.schur_high, r.schur_low), NN).reshape(2, 2, 8, size)
    solved = jnp.stack([solved[:, 0], solved[:, 1]], axis=0).reshape(2, 16, size)
    r.spare[...] = solved
    r.local[core] = r.spare[core]
    c_swap = channel()
    send(c_swap, r.spare.at[1 - core], r.local.at[core], partner)

    @pl.when(jnp.logical_not(has_before))
    def _():
        r.ahead_in[...] = jnp.zeros_like(r.ahead_in)

    @pl.when(jnp.logical_not(has_after))
    def _():
        r.back_in[...] = jnp.zeros_like(r.back_in)

    receive(c_swap, r.local.at[1 - core])
    start = r.local[1] - times(r.local[0], second, NT)
    c_start = channel()
    start_copy = send(c_start, r.start, r.start_in, mate, early)
    r.start[...] = start
    pl.when(early)(start_copy.start)

    receive(c_mate, r.twos.at[1 - role, core])
    send(c_pass, r.twos.at[1 - role, core], r.twos.at[1 - role, core], partner)
    receive(c_pass, r.twos.at[1 - role, 1 - core])
    split_two(1 - role)

    @pl.when(late)
    def _():
        receive(c_start, r.start_in)
        r.start[...] += times(r.start_in[...], two_late, NT)

    @pl.when(jnp.logical_or(has_before, early))
    def _():
        def merge_four(step, carry):
            at = pl.ds(pl.multiple_of(step * STRIP, STRIP), STRIP)
            merged = merged_rows(two_late, at, two_early)

            @pl.when(early)
            def _():
                for part in range(2):
                    r.four_high[part, at, :], r.four_low[part, at, :] = halves(merged[part])

            @pl.when(late)
            def _():
                for part in range(2):
                    r.four_high[part, :, at], r.four_low[part, :, at] = halves(merged[part].T)

            return carry

        lax.fori_loop(0, size // STRIP, merge_four, 0)

    c_late, c_early = channel(), channel()
    goes_on = jnp.logical_and(late, has_after)
    late_copy = send(c_late, r.ahead_out, r.ahead_in, next_late, goes_on)
    early_copy = send(c_early, r.ahead_out, r.ahead_in, next_early, goes_on)

    @pl.when(late)
    def _():
        @pl.when(has_before)
        def _():
            receive(c_late, r.ahead_in)
            r.ahead_out[...] = r.start[...] + times(r.ahead_in[...], four, NN)

        @pl.when(jnp.logical_not(has_before))
        def _():
            r.ahead_out[...] = r.start[...]

        @pl.when(has_after)
        def _():
            late_copy.start()
            early_copy.start()

        r.trace[1] = r.ahead_out[...]
        inner = r.start_in[...] + times(r.ahead_in[...], two_early, NT)
        r.trace[0] = r.local[0] - times(inner, first, NT)

    @pl.when(early)
    def _():
        pl.when(has_before)(lambda: receive(c_early, r.ahead_in))
        r.trace[0] = r.local[0] - times(r.ahead_in[...], first, NT)
        r.trace[1] = r.local[1] - times(r.trace[0], second, NT)

    queued = times(r.trace[0] - times(r.trace[1], second, NN), first, NN)
    r.queued[...] = queued
    c_queued = channel()
    queued_copy = send(c_queued, r.queued, r.queued_in, mate, late)
    pl.when(late)(queued_copy.start)

    c_back_early, c_back_late = channel(), channel()
    goes_back = jnp.logical_and(early, has_before)
    back_early = send(c_back_early, r.back_out, r.back_in, last_early, goes_back)
    back_late = send(c_back_late, r.back_out, r.back_in, last_late, goes_back)

    @pl.when(early)
    def _():
        receive(c_queued, r.queued_in)
        r.queued[...] += times(r.queued_in[...], two_early, NN)

        @pl.when(has_after)
        def _():
            receive(c_back_early, r.back_in)

        @pl.when(has_before)
        def _():
            r.back_out[...] = r.queued[...] + times(r.back_in[...], four, NN)
            back_early.start()
            back_late.start()

        r.carried[...] = r.queued_in[...] + times(r.back_in[...], two_late, NN)

    @pl.when(late)
    def _():
        pl.when(has_after)(lambda: receive(c_back_late, r.back_in))
        r.carried[...] = r.back_in[...]

    r.found[1] = r.trace[1] - r.carried[...]
    r.found[0] = r.trace[0] - times(r.found[1], second, NN)

    c_chip, c_far, c_across = channel(), channel(), channel()
    c_side = [[channel() for d in range(3)] for which in range(2)]
    place = r.gathered.at[sub, core]
    send(c_chip, r.found.at[1 - core], place, partner)
    send(c_far, r.found.at[core], place, opposite)
    send(c_across, r.found.at[1 - core], place, across)
    r.gathered[sub, core] = r.found[core]
    receive(c_chip, r.gathered.at[sub, 1 - core])
    for d in (1, 2, 3):
        send(c_side[0][d - 1], r.gathered.at[sub], r.gathered.at[sub], beside[d - 1])
    receive(c_far, r.gathered.at[other_sub, core])
    receive(c_across, r.gathered.at[other_sub, 1 - core])
    for d in (1, 2, 3):
        send(c_side[1][d - 1], r.gathered.at[other_sub], r.gathered.at[other_sub], beside[d - 1])
    for which in range(2):
        for d in (1, 2, 3):
            group = 2 * ((x + 4 - d) % 4) + (far if which == 0 else 1 - far)
            receive(c_side[which][d - 1], r.gathered.at[group])

    found = r.gathered[...].reshape(shots // 8, 2, 8, size)
    found = jnp.stack([found[:, 0], found[:, 1]], axis=0).reshape(2 * shots, size)
    r.found_high[...], r.found_low[...] = halves(found)
    turned = found.T
    r.separator_out[0] = turned[:, :shots]
    r.separator_out[1] = turned[:, shots:]

    def interior_of(b, carry):
        def product(left, high, low):
            left = halves(left)
            out = [dot3(left, (high[b, part], low[b, part])) for part in range(2)]
            return combine(out[0], out[1], 0)

        spread = r.spread[b]
        picked = dot(r.found_high[...], spread) + dot(r.found_low[...], spread)
        left = r.eliminated[b] - product(picked, r.coupling_high, r.coupling_low)
        turned = product(left, r.inverse_high, r.inverse_low).T
        r.interior_out[b, 0] = turned[:, :shots]
        r.interior_out[b, 1] = turned[:, shots:]
        return carry

    lax.fori_loop(0, blocks, interior_of, 0)

    for copy, when in unsent:
        if when is None:
            copy.wait_send()
        else:
            pl.when(when)(copy.wait_send)


CHANNELS = 32


def body(
    rhs_interior,
    rhs_separator,
    inverse_blocks,
    coupling,
    separator_rows,
    separator_inverse,
    transfer,
):
    _, nb, _, m, shots = rhs_interior.shape
    size = transfer.shape[-1]
    vmem = pltpu.VMEM
    inputs = {
        "rows": separator_rows[0][:, None, :],
        "rhs_hbm": rhs_interior[0],
        "separator_hbm": rhs_separator[0],
        "inverse_hbm": inverse_blocks[0],
        "coupling_hbm": coupling[0],
        "schur_hbm": separator_inverse[0],
        "transfer_hbm": transfer[0],
    }
    outputs = {
        "interior_out": jax.ShapeDtypeStruct((nb, 2, m, shots), F32),
        "separator_out": jax.ShapeDtypeStruct((2, size, shots), F32),
    }
    scratch = {
        "inverse": vmem((nb, 2, m, m), F32),
        "inverse_high": vmem((nb, 2, m, m), BF16),
        "inverse_low": vmem((nb, 2, m, m), BF16),
        "rhs": vmem((nb, 2, m, shots), F32),
        "coupling": vmem((nb, 2, size, m), F32),
        "coupling_high": vmem((nb, 2, size, m), BF16),
        "coupling_low": vmem((nb, 2, size, m), BF16),
        "spread": vmem((nb, size, size), BF16),
        "eliminated": vmem((nb, 2 * shots, m), F32),
        "given": vmem((2, size, shots), F32),
        "total": vmem((size, 2 * shots), F32),
        "load": vmem((8, 32, size), F32),
        "from_x": vmem((2, 3, 32, size), F32),
        "forward_sum": vmem((32, size), F32),
        "from_z": vmem((32, size), F32),
        "schur": vmem((2, size, size), F32),
        "schur_high": vmem((2, size, size), BF16),
        "schur_low": vmem((2, size, size), BF16),
        "pair": vmem((2, 2, size, size), F32),
        "pair_high": vmem((2, 2, size, size), BF16),
        "pair_low": vmem((2, 2, size, size), BF16),
        "twos": vmem((2, 2, 2, size // 2, size), F32),
        "two_high": vmem((2, 2, size, size), BF16),
        "two_low": vmem((2, 2, size, size), BF16),
        "four_high": vmem((2, size, size), BF16),
        "four_low": vmem((2, size, size), BF16),
        "spare": vmem((2, 16, size), F32),
        "local": vmem((2, 16, size), F32),
        "start": vmem((16, size), F32),
        "start_in": vmem((16, size), F32),
        "ahead_in": vmem((16, size), F32),
        "ahead_out": vmem((16, size), F32),
        "trace": vmem((2, 16, size), F32),
        "queued": vmem((16, size), F32),
        "queued_in": vmem((16, size), F32),
        "back_in": vmem((16, size), F32),
        "back_out": vmem((16, size), F32),
        "carried": vmem((16, size), F32),
        "found": vmem((2, 16, size), F32),
        "gathered": vmem((8, 2, 16, size), F32),
        "found_high": vmem((2 * shots, size), BF16),
        "found_low": vmem((2 * shots, size), BF16),
        "send_sem": pltpu.SemaphoreType.DMA((CHANNELS,)),
        "recv_sem": pltpu.SemaphoreType.DMA((CHANNELS,)),
        "here_sem": pltpu.SemaphoreType.DMA((3,)),
        "block_sem": pltpu.SemaphoreType.DMA((3, nb)),
    }
    names = list(inputs) + list(outputs) + list(scratch)

    def sweep_kernel(*refs):
        kernel(names, *refs)

    interior, separator = pl.pallas_call(
        sweep_kernel,
        out_shape=tuple(outputs.values()),
        in_specs=[pl.BlockSpec(memory_space=pltpu.VMEM)]
        + [pl.BlockSpec(memory_space=pl.ANY)] * (len(inputs) - 1),
        out_specs=(pl.BlockSpec(memory_space=pltpu.VMEM),) * 2,
        scratch_shapes=list(scratch.values()),
        compiler_params=pltpu.CompilerParams(
            collective_id=0, has_side_effects=True, vmem_limit_bytes=60 << 20
        ),
    )(*inputs.values())
    return (interior[None], separator[None])


def solution(mesh):
    in_specs = (
        P("slab", "sub", None, None, None),
        P("slab", None, None, None),
        P("slab", "sub", None, None, None),
        P("slab", "sub", None, None, None),
        P("slab", "sub", None),
        P("slab", None, None, None),
        P("slab", None, None, None),
    )
    out_specs = (P("slab", "sub", None, None, None), P("slab", None, None, None))
    return jax.shard_map(body, mesh=mesh, in_specs=in_specs, out_specs=out_specs, check_vma=False)
```

time: 1180 us -> 141 us (0.12); the launches traced: 1170 us -> 141 us
  waiting for transfers between devices: 825 us -> 0 us
  starting transfers between devices: 251 us -> 0 us
  Pallas kernels: 0 us -> 136 us
  matrix products: 59 us -> 0 us
  between operations: 14.8 us -> 0.65 us
    ppermute x64 -> x0, waiting for transfers between devices: 718 us -> none  [from_behind(): lax.ppermute(value, axis, [(source, source + steps) for source in range(f...]
    ppermute x64 -> x0, starting transfers between devices: 251 us -> none  [from_behind(): lax.ppermute(value, axis, [(source, source + steps) for source in range(f...]
    pallas_call x0 -> x1, Pallas kernels: none -> 136 us  [body(): pl.pallas_call(sweep_kernel, out_shape=tuple(outputs.values()), in_specs=...]
    psum x1 -> x0, waiting for transfers between devices: 107 us -> none  [body(): separator_load = lax.psum(partial_load, 'sub')]
    dot_general x29 -> x0, matrix products: 59 us -> none  [the longest x28 54.9 us: multiply(): return jnp.matmul(left, right, precision=HIGH)]
  transfers between devices with their start and end apart: 65 -> 0, of which waited for: 65 -> 0; matrix products, arithmetic and copies ran while one was open for 0% -> 0% of each run, Pallas kernels for 0% -> 0%
where the time goes in v2:
time: 141 us
  Pallas kernels  136 us (96%)
  local copies, waits for them, and re-layouts  4.43 us (3%)
    pallas_call x1, Pallas kernels, body(): pl.pallas_call(sweep_kernel, out_shape=tuple(outputs.values()), in_specs=...  136 us
    unnamed x4, local copies, waits for them, and re-layouts  3.12 us

profile of v2, /device:TPU:1, one launch (start us, length us, event | category | flops | bytes accessed | tf_op | source)
XLA Modules:
  0.0 141.0 jit_solution(168334971932369128)
XLA Ops:
  0.6 1.3 broadcast_in_dim_squeeze.3.refs_0_
  1.9 135.9 %shard_map.86 = (f32[4,2,256,128]{3,2,1,0:T(8,128)}, f32[2,512,128]{2,1,0:T(8,128)}) custom-call(s32[4,1,512]{2,1,0:T(1,128)} %broadcast_in_dim_squeeze.3.refs_0_, f32[4,2,256,128]{3,2,1,0:T(8,128)} %bitcast.12, f32[2,512,128]{2,1,0:T(8,128)} %bitcast.14, f32[4,2,256,256]{3,2,1,0:T(8,128)} %bitcast.9, f32[4,2,512,256]{3,2,1,0:T(8,128)} %bitcast.8, ...), custom_call_target="tpu_custom_call" | custom-call | tf_op jit(solution)/shard_map/pallas_call | solution.py:518
  137.8 0.0 copy-start
  137.8 2.3 %copy.11 = f32[1,4,2,256,128]{4,3,2,1,0:T(8,128)} copy(f32[1,4,2,256,128]{4,3,2,1,0:T(8,128)} %bitcast.13) | data formatting | bytes 2097152
  140.2 0.0 copy-done
  140.2 0.8 copy.12
Async XLA Ops:
  137.8 2.3 %copy-start = (f32[2,512,128]{2,1,0:T(8,128)S(1)}, f32[2,512,128]{2,1,0:T(8,128)}, u32[]{:S(2)}) copy-start(f32[2,512,128]{2,1,0:T(8,128)} %get-tuple-element.5) | copy-start | bytes 1572868

commit v3 on v2

--- a/solution.py
+++ b/solution.py
@@ -24,9 +24,10 @@
     return lax.dot_general(left, right, dims, preferred_element_type=F32)
 
 
-def dot3(left, right, dims=NN):
-    return dot(left[0], right[0], dims) + (
-        dot(left[0], right[1], dims) + dot(left[1], right[0], dims)
+def dot3(left, right):
+    return dot(
+        jnp.concatenate([left[0], left[0], left[1]], axis=1),
+        jnp.concatenate([right[0], right[1], right[0]], axis=0),
     )
 
 
@@ -103,6 +104,15 @@
     own_schur = pltpu.make_async_copy(r.schur_hbm, r.schur, r.here_sem.at[2])
     own_transfer.start()
 
+    r.total[...] = jnp.zeros_like(r.total)
+
+    def spread_of(b, carry):
+        for i in range(size // STRIP):
+            at = slice(i * STRIP, (i + 1) * STRIP)
+            place = lax.broadcasted_iota(jnp.int32, (STRIP, size), 0) + i * STRIP
+            r.spread[b, at] = (place == r.rows[pl.ds(b, 1), :]).astype(BF16)
+        return carry
+
     barrier = pltpu.get_barrier_semaphore()
 
     def greet(device):
@@ -137,6 +147,7 @@
     own_given.start()
     own_schur.start()
 
+    lax.fori_loop(0, blocks, spread_of, 0)
     own_transfer.wait()
     receive(c_transfer, r.pair.at[1 - core])
 
@@ -160,19 +171,26 @@
         return out[0][:STRIP] - out[1][STRIP:], out[0][STRIP:] + out[1][:STRIP]
 
     half = size // 2
+    strips = half // STRIP
 
     def merge_two(step, carry):
         at = pl.ds(pl.multiple_of(core * half + step * STRIP, STRIP), STRIP)
-        to = pl.ds(pl.multiple_of(step * STRIP, STRIP), STRIP)
         merged = merged_rows(second, at, first)
         for part in range(2):
-            r.twos[role, core, part, to, :] = merged[part]
+            r.twos[role, strips * core + step, part] = merged[part]
         return carry
 
     lax.fori_loop(0, half // STRIP, merge_two, 0)
-    c_half, c_mate, c_pass = channel(), channel(), channel()
-    send(c_mate, r.twos.at[role, core], r.twos.at[role, core], mate)
-    send(c_half, r.twos.at[role, core], r.twos.at[role, core], partner)
+    c_half = channel()
+    c_mate, c_pass = [[channel() for i in range(strips)] for j in range(2)]
+    halved = r.twos.at[role, pl.ds(strips * core, strips)]
+    send(c_half, halved, halved, partner)
+
+    def send_mate(i):
+        piece = r.twos.at[role, strips * core + i]
+        send(c_mate[i], piece, piece, mate)
+
+    send_mate(0)
 
     def combine(real, imag, axis):
         n = real.shape[axis] // 2
@@ -182,31 +200,39 @@
             )
         return jnp.concatenate([real[:n] - imag[n:], real[n:] + imag[:n]], axis=0)
 
-    r.total[...] = jnp.zeros_like(r.total)
-
     def load_of(b, carry):
         for copy in local_copies(b):
             copy.wait()
-        for source, high, low in (
-            (r.inverse, r.inverse_high, r.inverse_low),
-            (r.coupling, r.coupling_high, r.coupling_low),
-        ):
+        r.rhs_high[...], r.rhs_low[...] = halves(
+            jnp.concatenate([r.rhs[b, 0], r.rhs[b, 1]], axis=1)
+        )
+
+        def strip(at, source, high, low, right):
+            out = []
             for part in range(2):
-                high[b, part], low[b, part] = halves(source[b, part])
-
-        def product(high, low, right):
-            right = halves(right)
-            out = [dot3((high[b, part], low[b, part]), right) for part in range(2)]
+                left = halves(source[b, part, at])
+                high[b, part, at], low[b, part, at] = left
+                out.append(dot3(left, right))
             return combine(out[0], out[1], 1)
 
-        eliminated = product(
-            r.inverse_high, r.inverse_low, jnp.concatenate([r.rhs[b, 0], r.rhs[b, 1]], axis=1)
-        )
-        r.eliminated[b] = eliminated.T
-        weighted = halves(product(r.coupling_high, r.coupling_low, eliminated))
-        spread = (lax.broadcasted_iota(jnp.int32, (size, size), 0) == r.rows[b]).astype(BF16)
-        r.spread[b] = spread
-        r.total[...] += dot(spread, weighted[0]) + dot(spread, weighted[1])
+        for i in range(m // STRIP):
+            at = slice(i * STRIP, (i + 1) * STRIP)
+            right = (r.rhs_high[...], r.rhs_low[...])
+            value = strip(at, r.inverse, r.inverse_high, r.inverse_low, right)
+            r.eliminated[b, at] = value
+            r.known_high[at], r.known_low[at] = halves(value)
+        for i in range(size // STRIP):
+            at = slice(i * STRIP, (i + 1) * STRIP)
+            right = (r.known_high[...], r.known_low[...])
+            value = strip(at, r.coupling, r.coupling_high, r.coupling_low, right)
+            r.weighted_high[at], r.weighted_low[at] = halves(value)
+        for i in range(size // STRIP):
+            at = slice(i * STRIP, (i + 1) * STRIP)
+            spread = r.spread[b, at]
+            r.total[at] += dot(
+                jnp.concatenate([spread, spread], axis=1),
+                jnp.concatenate([r.weighted_high[...], r.weighted_low[...]], axis=0),
+            )
         return carry
 
     lax.fori_loop(0, blocks, load_of, 0)
@@ -242,17 +268,18 @@
 
     r.forward_sum[...] = side_sum(0, other_sub)
     send(c_z, r.forward_sum, r.from_z, opposite)
+    for i in range(1, strips):
+        send_mate(i)
     own_sum = side_sum(1, sub)
 
-    receive(c_half, r.twos.at[role, 1 - core])
+    receive(c_half, r.twos.at[role, pl.ds(strips * (1 - core), strips)])
 
     def split_two(which):
         def step_of(step, carry):
-            piece, at = step // 2, pl.ds(pl.multiple_of((step % 2) * STRIP, STRIP), STRIP)
             to = pl.ds(pl.multiple_of(step * STRIP, STRIP), STRIP)
             for part in range(2):
                 r.two_high[which, part, to, :], r.two_low[which, part, to, :] = halves(
-                    r.twos[which, piece, part, at, :]
+                    r.twos[which, step, part]
                 )
             return carry
 
@@ -288,17 +315,31 @@
     r.start[...] = start
     pl.when(early)(start_copy.start)
 
-    receive(c_mate, r.twos.at[1 - role, core])
-    send(c_pass, r.twos.at[1 - role, core], r.twos.at[1 - role, core], partner)
-    receive(c_pass, r.twos.at[1 - role, 1 - core])
-    split_two(1 - role)
+    c_late, c_early = channel(), channel()
+    goes_on = jnp.logical_and(late, has_after)
+    late_copy = send(c_late, r.ahead_out, r.ahead_in, next_late, goes_on)
+    early_copy = send(c_early, r.ahead_out, r.ahead_in, next_early, goes_on)
 
     @pl.when(late)
     def _():
         receive(c_start, r.start_in)
         r.start[...] += times(r.start_in[...], two_late, NT)
 
-    @pl.when(jnp.logical_or(has_before, early))
+        @pl.when(jnp.logical_not(has_before))
+        def _():
+            r.ahead_out[...] = r.start[...]
+            late_copy.start()
+            early_copy.start()
+
+    for i in range(strips):
+        piece = r.twos.at[1 - role, strips * core + i]
+        receive(c_mate[i], piece)
+        send(c_pass[i], piece, piece, partner)
+    for i in range(strips):
+        receive(c_pass[i], r.twos.at[1 - role, strips * (1 - core) + i])
+    split_two(1 - role)
+
+    @pl.when(has_before)
     def _():
         def merge_four(step, carry):
             at = pl.ds(pl.multiple_of(step * STRIP, STRIP), STRIP)
@@ -318,10 +359,38 @@
 
         lax.fori_loop(0, size // STRIP, merge_four, 0)
 
-    c_late, c_early = channel(), channel()
-    goes_on = jnp.logical_and(late, has_after)
-    late_copy = send(c_late, r.ahead_out, r.ahead_in, next_late, goes_on)
-    early_copy = send(c_early, r.ahead_out, r.ahead_in, next_early, goes_on)
+    def weights_of(b, carry):
+        spread = r.spread[b]
+        for part in range(2):
+            r.placed_high[part] = dot(spread, r.coupling_high[b, part]).astype(BF16)
+            r.placed_low[part] = dot(spread, r.coupling_low[b, part]).astype(BF16)
+
+        def inverse(part):
+            return r.inverse_high[b, part], r.inverse_low[b, part]
+
+        def strip_of(step, carry):
+            at = pl.ds(pl.multiple_of(step * STRIP, STRIP), STRIP)
+            left = [
+                jnp.concatenate([source[0, at, :], source[1, at, :]], axis=0)
+                for source in (r.placed_high, r.placed_low)
+            ]
+            merged = combine(dot3(left, inverse(0)), dot3(left, inverse(1)), 0)
+            for part in range(2):
+                r.coupling_high[b, part, at, :], r.coupling_low[b, part, at, :] = halves(
+                    merged[part * STRIP : (part + 1) * STRIP]
+                )
+            return carry
+
+        lax.fori_loop(0, size // STRIP, strip_of, 0)
+        left = halves(r.eliminated[b].T)
+        r.eliminated[b] = combine(dot3(left, inverse(0)), dot3(left, inverse(1)), 0)
+        return carry
+
+    towards_end = duo >= duos - 2
+
+    @pl.when(towards_end)
+    def _():
+        lax.fori_loop(0, blocks, weights_of, 0)
 
     @pl.when(late)
     def _():
@@ -330,14 +399,10 @@
             receive(c_late, r.ahead_in)
             r.ahead_out[...] = r.start[...] + times(r.ahead_in[...], four, NN)
 
-        @pl.when(jnp.logical_not(has_before))
-        def _():
-            r.ahead_out[...] = r.start[...]
-
-        @pl.when(has_after)
-        def _():
-            late_copy.start()
-            early_copy.start()
+            @pl.when(has_after)
+            def _():
+                late_copy.start()
+                early_copy.start()
 
         r.trace[1] = r.ahead_out[...]
         inner = r.start_in[...] + times(r.ahead_in[...], two_early, NT)
@@ -354,6 +419,10 @@
     c_queued = channel()
     queued_copy = send(c_queued, r.queued, r.queued_in, mate, late)
     pl.when(late)(queued_copy.start)
+
+    @pl.when(jnp.logical_not(towards_end))
+    def _():
+        lax.fori_loop(0, blocks, weights_of, 0)
 
     c_back_early, c_back_late = channel(), channel()
     goes_back = jnp.logical_and(early, has_before)
@@ -412,15 +481,11 @@
     r.separator_out[1] = turned[:, shots:]
 
     def interior_of(b, carry):
-        def product(left, high, low):
-            left = halves(left)
-            out = [dot3(left, (high[b, part], low[b, part])) for part in range(2)]
-            return combine(out[0], out[1], 0)
-
-        spread = r.spread[b]
-        picked = dot(r.found_high[...], spread) + dot(r.found_low[...], spread)
-        left = r.eliminated[b] - product(picked, r.coupling_high, r.coupling_low)
-        turned = product(left, r.inverse_high, r.inverse_low).T
+        left = (r.found_high[...], r.found_low[...])
+        out = [
+            dot3(left, (r.coupling_high[b, part], r.coupling_low[b, part])) for part in range(2)
+        ]
+        turned = (r.eliminated[b] - combine(out[0], out[1], 0)).T
         r.interior_out[b, 0] = turned[:, :shots]
         r.interior_out[b, 1] = turned[:, shots:]
         return carry
@@ -450,7 +515,7 @@
     size = transfer.shape[-1]
     vmem = pltpu.VMEM
     inputs = {
-        "rows": separator_rows[0][:, None, :],
+        "rows": separator_rows[0],
         "rhs_hbm": rhs_interior[0],
         "separator_hbm": rhs_separator[0],
         "inverse_hbm": inverse_blocks[0],
@@ -471,7 +536,15 @@
         "coupling_high": vmem((nb, 2, size, m), BF16),
         "coupling_low": vmem((nb, 2, size, m), BF16),
         "spread": vmem((nb, size, size), BF16),
-        "eliminated": vmem((nb, 2 * shots, m), F32),
+        "placed_high": vmem((2, size, m), BF16),
+        "placed_low": vmem((2, size, m), BF16),
+        "eliminated": vmem((nb, m, 2 * shots), F32),
+        "rhs_high": vmem((m, 2 * shots), BF16),
+        "rhs_low": vmem((m, 2 * shots), BF16),
+        "known_high": vmem((m, 2 * shots), BF16),
+        "known_low": vmem((m, 2 * shots), BF16),
+        "weighted_high": vmem((size, 2 * shots), BF16),
+        "weighted_low": vmem((size, 2 * shots), BF16),
         "given": vmem((2, size, shots), F32),
         "total": vmem((size, 2 * shots), F32),
         "load": vmem((8, 32, size), F32),
@@ -484,7 +557,7 @@
         "pair": vmem((2, 2, size, size), F32),
         "pair_high": vmem((2, 2, size, size), BF16),
         "pair_low": vmem((2, 2, size, size), BF16),
-        "twos": vmem((2, 2, 2, size // 2, size), F32),
+        "twos": vmem((2, size // STRIP, 2, STRIP, size), F32),
         "two_high": vmem((2, 2, size, size), BF16),
         "two_low": vmem((2, 2, size, size), BF16),
         "four_high": vmem((2, size, size), BF16),
@@ -519,11 +592,11 @@
         sweep_kernel,
         out_shape=tuple(outputs.values()),
         in_specs=[pl.BlockSpec(memory_space=pltpu.VMEM)]
-        + [pl.BlockSpec(memory_space=pl.ANY)] * (len(inputs) - 1),
+        + [pl.BlockSpec(memory_space=pltpu.HBM)] * (len(inputs) - 1),
         out_specs=(pl.BlockSpec(memory_space=pltpu.VMEM),) * 2,
         scratch_shapes=list(scratch.values()),
         compiler_params=pltpu.CompilerParams(
-            collective_id=0, has_side_effects=True, vmem_limit_bytes=60 << 20
+            collective_id=0, has_side_effects=True, vmem_limit_bytes=61 << 20
         ),
     )(*inputs.values())
     return (interior[None], separator[None])

time: 141 us -> 130 us (0.922)
  Pallas kernels: 136 us -> 126 us
    pallas_call x1, Pallas kernels: 136 us -> 126 us  [body(): pl.pallas_call(sweep_kernel, out_shape=tuple(outputs.values()), in_specs=...]
where the time goes in v3:
time: 130 us
  Pallas kernels  126 us (97%)
  local copies, waits for them, and re-layouts  3.12 us (2%)
    pallas_call x1, Pallas kernels, body(): pl.pallas_call(sweep_kernel, out_shape=tuple(outputs.values()), in_specs=...  126 us
    unnamed x4, local copies, waits for them, and re-layouts  3.12 us

profile of v3, /device:TPU:1, one launch (start us, length us, event | category | flops | bytes accessed | tf_op | source)
XLA Modules:
  0.0 129.9 jit_solution(3301331241610965468)
XLA Ops:
  0.6 126.1 %shard_map.86 = (f32[4,2,256,128]{3,2,1,0:T(8,128)}, f32[2,512,128]{2,1,0:T(8,128)}) custom-call(s32[4,512]{1,0:T(4,128)} %bitcast.17, f32[4,2,256,128]{3,2,1,0:T(8,128)} %bitcast.13, f32[2,512,128]{2,1,0:T(8,128)} %bitcast.15, f32[4,2,256,256]{3,2,1,0:T(8,128)} %bitcast.10, f32[4,2,512,256]{3,2,1,0:T(8,128)} %bitcast.9, f32[2,512,512]{2,1,0:T(8,128)} %bitcast.11, ...), custom_call_target="tpu_custom_call" | custom-call | tf_op jit(solution)/shard_map/pallas_call | solution.py:591
  126.7 0.0 copy-start
  126.7 2.3 %copy.11 = f32[1,4,2,256,128]{4,3,2,1,0:T(8,128)} copy(f32[1,4,2,256,128]{4,3,2,1,0:T(8,128)} %bitcast.14) | data formatting | bytes 2097152
  129.1 0.0 copy-done
  129.1 0.8 copy.12
Async XLA Ops:
  126.7 2.3 %copy-start = (f32[2,512,128]{2,1,0:T(8,128)S(1)}, f32[2,512,128]{2,1,0:T(8,128)}, u32[]{:S(2)}) copy-start(f32[2,512,128]{2,1,0:T(8,128)} %get-tuple-element.5) | copy-start | bytes 1572868

commit v4 on v3

--- a/solution.py
+++ b/solution.py
@@ -53,6 +53,12 @@
     after, before = (2 * duos - 3 - duo) // (duos - 1), (duo + duos - 2) // (duos - 1)
     has_after, has_before = duo < duos - 1, duo > 0
     early, late = role == 0, role == 1
+    row, upper = duo // 2, duo % 2
+    rows = duos // 2
+    row_after, row_before = (2 * rows - 3 - row) // (rows - 1), (row + rows - 2) // (rows - 1)
+    has_row_after, has_row_before = row < rows - 1, row > 0
+    leads = jnp.logical_and(early, upper == 0)
+    helps = jnp.logical_and(early, upper == 1)
     blocks, _, size, m = r.coupling_hbm.shape
     shots = r.rhs_hbm.shape[-1]
 
@@ -64,6 +70,7 @@
     beside = [(slab, ((x + d) % 4) * 2 + far) for d in (1, 2, 3)]
     next_late, next_early = ((slab + 4) % slabs, sub), ((slab + 2) % slabs, sub)
     last_early, last_late = ((slab + slabs - 4) % slabs, sub), ((slab + slabs - 2) % slabs, sub)
+    next_lead, last_lead = ((slab + 8) % slabs, sub), ((slab + slabs - 8) % slabs, sub)
 
     count = [0]
     unsent = []
@@ -137,7 +144,23 @@
         def _():
             greet(last_late)
 
-    pl.semaphore_wait(barrier, 7 + after + before + role * after + (1 - role) * before)
+    @pl.when(jnp.logical_and(leads, has_row_after))
+    def _():
+        greet(next_lead)
+
+    @pl.when(jnp.logical_and(leads, has_row_before))
+    def _():
+        greet(last_lead)
+
+    pl.semaphore_wait(
+        barrier,
+        7
+        + after
+        + before
+        + role * after
+        + (1 - role) * before
+        + (1 - role) * (1 - upper) * (row_after + row_before),
+    )
 
     c_transfer = channel()
     send(c_transfer, r.transfer_hbm, r.pair.at[core], partner)
@@ -339,7 +362,7 @@
         receive(c_pass[i], r.twos.at[1 - role, strips * (1 - core) + i])
     split_two(1 - role)
 
-    @pl.when(has_before)
+    @pl.when(jnp.logical_and(duo > 1, jnp.logical_or(late, upper == 0)))
     def _():
         def merge_four(step, carry):
             at = pl.ds(pl.multiple_of(step * STRIP, STRIP), STRIP)
@@ -358,6 +381,24 @@
             return carry
 
         lax.fori_loop(0, size // STRIP, merge_four, 0)
+
+    gives = jnp.logical_and(helps, has_row_after)
+    takes = jnp.logical_and(leads, has_row_after)
+    c_four, c_four_pass = channel(), channel()
+    half_four = pl.ds(strips * core, strips)
+    four_copy = send(c_four, r.four_out, r.four_in.at[half_four], last_early, gives)
+
+    @pl.when(gives)
+    def _():
+        def merge_half(step, carry):
+            at = pl.ds(pl.multiple_of(core * half + step * STRIP, STRIP), STRIP)
+            merged = merged_rows(two_late, at, two_early)
+            for part in range(2):
+                r.four_out[step, part] = merged[part]
+            return carry
+
+        lax.fori_loop(0, strips, merge_half, 0)
+        four_copy.start()
 
     def weights_of(b, carry):
         spread = r.spread[b]
@@ -397,7 +438,16 @@
         @pl.when(has_before)
         def _():
             receive(c_late, r.ahead_in)
-            r.ahead_out[...] = r.start[...] + times(r.ahead_in[...], four, NN)
+
+            @pl.when(duo > 1)
+            def _():
+                r.ahead_out[...] = r.start[...] + times(r.ahead_in[...], four, NN)
+
+            @pl.when(duo == 1)
+            def _():
+                r.ahead_out[...] = r.start[...] + times(
+                    times(r.ahead_in[...], two_early, NT), two_late, NT
+                )
 
             @pl.when(has_after)
             def _():
@@ -424,32 +474,76 @@
     def _():
         lax.fori_loop(0, blocks, weights_of, 0)
 
-    c_back_early, c_back_late = channel(), channel()
-    goes_back = jnp.logical_and(early, has_before)
-    back_early = send(c_back_early, r.back_out, r.back_in, last_early, goes_back)
+    c_upper, c_lower, c_lead, c_help, c_back_late = [channel() for i in range(5)]
+    goes_back = jnp.logical_and(leads, has_row_before)
+    upper_copy = send(c_upper, r.queued, r.upper_in, last_early, helps)
+    lower_copy = send(c_lower, r.lower, r.lower_in, mate, leads)
+    back_lead = send(c_lead, r.back_out, r.back_in, last_lead, goes_back)
+    back_help = send(c_help, r.back_out, r.back_in, last_early, goes_back)
     back_late = send(c_back_late, r.back_out, r.back_in, last_late, goes_back)
+    pass_copy = send(
+        c_four_pass, r.four_in.at[half_four], r.four_in.at[half_four], partner, takes
+    )
+    top = (r.top_high, r.top_low)
 
     @pl.when(early)
     def _():
         receive(c_queued, r.queued_in)
         r.queued[...] += times(r.queued_in[...], two_early, NN)
 
-        @pl.when(has_after)
+    @pl.when(helps)
+    def _():
+        upper_copy.start()
+        pl.when(has_row_after)(lambda: receive(c_help, r.back_in))
+        r.carried[...] = r.queued_in[...] + times(r.back_in[...], two_late, NN)
+
+    @pl.when(leads)
+    def _():
+        @pl.when(has_row_after)
         def _():
-            receive(c_back_early, r.back_in)
-
-        @pl.when(has_before)
+            receive(c_four, r.four_in.at[half_four])
+            pass_copy.start()
+            receive(c_four_pass, r.four_in.at[pl.ds(strips * (1 - core), strips)])
+
+            def split_top(step, carry):
+                to = pl.ds(pl.multiple_of(step * STRIP, STRIP), STRIP)
+                for part in range(2):
+                    r.top_high[part, to, :], r.top_low[part, to, :] = halves(r.four_in[step, part])
+                return carry
+
+            lax.fori_loop(0, size // STRIP, split_top, 0)
+
+        receive(c_upper, r.upper_in)
+
+        @pl.when(has_row_after)
         def _():
-            r.back_out[...] = r.queued[...] + times(r.back_in[...], four, NN)
-            back_early.start()
+            receive(c_lead, r.back_in)
+            r.lower[...] = r.upper_in[...] + times(r.back_in[...], top, NN)
+
+        @pl.when(jnp.logical_not(has_row_after))
+        def _():
+            r.lower[...] = r.upper_in[...]
+
+        lower_copy.start()
+
+        @pl.when(has_row_before)
+        def _():
+            r.back_out[...] = r.queued[...] + times(r.lower[...], four, NN)
+            back_lead.start()
+            back_help.start()
             back_late.start()
 
-        r.carried[...] = r.queued_in[...] + times(r.back_in[...], two_late, NN)
-
-    @pl.when(late)
-    def _():
-        pl.when(has_after)(lambda: receive(c_back_late, r.back_in))
+        r.carried[...] = r.queued_in[...] + times(r.lower[...], two_late, NN)
+
+    @pl.when(jnp.logical_and(late, upper == 1))
+    def _():
+        pl.when(has_row_after)(lambda: receive(c_back_late, r.back_in))
         r.carried[...] = r.back_in[...]
+
+    @pl.when(jnp.logical_and(late, upper == 0))
+    def _():
+        receive(c_lower, r.lower_in)
+        r.carried[...] = r.lower_in[...]
 
     r.found[1] = r.trace[1] - r.carried[...]
     r.found[0] = r.trace[0] - times(r.found[1], second, NN)
@@ -499,7 +593,7 @@
             pl.when(when)(copy.wait_send)
 
 
-CHANNELS = 32
+CHANNELS = 40
 
 
 def body(
@@ -562,6 +656,13 @@
         "two_low": vmem((2, 2, size, size), BF16),
         "four_high": vmem((2, size, size), BF16),
         "four_low": vmem((2, size, size), BF16),
+        "four_out": vmem((size // STRIP // 2, 2, STRIP, size), F32),
+        "four_in": vmem((size // STRIP, 2, STRIP, size), F32),
+        "top_high": vmem((2, size, size), BF16),
+        "top_low": vmem((2, size, size), BF16),
+        "upper_in": vmem((16, size), F32),
+        "lower": vmem((16, size), F32),
+        "lower_in": vmem((16, size), F32),
         "spare": vmem((2, 16, size), F32),
         "local": vmem((2, 16, size), F32),
         "start": vmem((16, size), F32),

time: 130 us -> 114 us (0.88)
  Pallas kernels: 126 us -> 109 us
    pallas_call x1, Pallas kernels: 126 us -> 109 us  [body(): pl.pallas_call(sweep_kernel, out_shape=tuple(outputs.values()), in_specs=...]
where the time goes in v4:
time: 114 us; the launch traced here: 113 us
  Pallas kernels  109 us (96%)
  local copies, waits for them, and re-layouts  3.12 us (3%)
    pallas_call x1, Pallas kernels, body(): pl.pallas_call(sweep_kernel, out_shape=tuple(outputs.values()), in_specs=...  109 us
    unnamed x4, local copies, waits for them, and re-layouts  3.12 us

profile of v4, /device:TPU:1, one launch (start us, length us, event | category | flops | bytes accessed | tf_op | source)
XLA Modules:
  0.0 113.2 jit_solution(14708788022720989652)
XLA Ops:
  0.6 109.4 %shard_map.86 = (f32[4,2,256,128]{3,2,1,0:T(8,128)}, f32[2,512,128]{2,1,0:T(8,128)}) custom-call(s32[4,512]{1,0:T(4,128)} %bitcast.17, f32[4,2,256,128]{3,2,1,0:T(8,128)} %bitcast.13, f32[2,512,128]{2,1,0:T(8,128)} %bitcast.15, f32[4,2,256,256]{3,2,1,0:T(8,128)} %bitcast.10, f32[4,2,512,256]{3,2,1,0:T(8,128)} %bitcast.9, f32[2,512,512]{2,1,0:T(8,128)} %bitcast.11, ...), custom_call_target="tpu_custom_call" | custom-call | tf_op jit(solution)/shard_map/pallas_call | solution.py:692
  110.1 0.0 copy-start
  110.1 2.3 %copy.11 = f32[1,4,2,256,128]{4,3,2,1,0:T(8,128)} copy(f32[1,4,2,256,128]{4,3,2,1,0:T(8,128)} %bitcast.14) | data formatting | bytes 2097152
  112.4 0.0 copy-done
  112.4 0.8 copy.12
Async XLA Ops:
  110.1 2.3 %copy-start = (f32[2,512,128]{2,1,0:T(8,128)S(1)}, f32[2,512,128]{2,1,0:T(8,128)}, u32[]{:S(2)}) copy-start(f32[2,512,128]{2,1,0:T(8,128)} %get-tuple-element.5) | copy-start | bytes 1572868

commit v5 on v4

--- a/solution.py
+++ b/solution.py
@@ -107,9 +107,12 @@
         ]
 
     own_transfer = pltpu.make_async_copy(r.transfer_hbm, r.pair.at[core], r.here_sem.at[0])
-    own_given = pltpu.make_async_copy(r.separator_hbm, r.given, r.here_sem.at[1])
-    own_schur = pltpu.make_async_copy(r.schur_hbm, r.schur, r.here_sem.at[2])
+    own_schur = pltpu.make_async_copy(r.schur_hbm, r.schur, r.here_sem.at[1])
     own_transfer.start()
+    for b in range(blocks):
+        for copy in local_copies(b):
+            copy.start()
+    own_schur.start()
 
     r.total[...] = jnp.zeros_like(r.total)
 
@@ -164,56 +167,6 @@
 
     c_transfer = channel()
     send(c_transfer, r.transfer_hbm, r.pair.at[core], partner)
-    for b in range(blocks):
-        for copy in local_copies(b):
-            copy.start()
-    own_given.start()
-    own_schur.start()
-
-    lax.fori_loop(0, blocks, spread_of, 0)
-    own_transfer.wait()
-    receive(c_transfer, r.pair.at[1 - core])
-
-    def split_pair(step, carry):
-        at = pl.ds(pl.multiple_of(step * STRIP, STRIP), STRIP)
-        for slot in range(2):
-            for part in range(2):
-                r.pair_high[slot, part, at, :], r.pair_low[slot, part, at, :] = halves(
-                    r.pair[slot, part, at, :]
-                )
-        return carry
-
-    lax.fori_loop(0, size // STRIP, split_pair, 0)
-    first = (r.pair_high.at[0], r.pair_low.at[0])
-    second = (r.pair_high.at[1], r.pair_low.at[1])
-
-    def merged_rows(left, at, right):
-        rows_high = jnp.concatenate([left[0][0, at, :], left[0][1, at, :]], axis=0)
-        rows_low = jnp.concatenate([left[1][0, at, :], left[1][1, at, :]], axis=0)
-        out = [dot3((rows_high, rows_low), (right[0][part], right[1][part])) for part in range(2)]
-        return out[0][:STRIP] - out[1][STRIP:], out[0][STRIP:] + out[1][:STRIP]
-
-    half = size // 2
-    strips = half // STRIP
-
-    def merge_two(step, carry):
-        at = pl.ds(pl.multiple_of(core * half + step * STRIP, STRIP), STRIP)
-        merged = merged_rows(second, at, first)
-        for part in range(2):
-            r.twos[role, strips * core + step, part] = merged[part]
-        return carry
-
-    lax.fori_loop(0, half // STRIP, merge_two, 0)
-    c_half = channel()
-    c_mate, c_pass = [[channel() for i in range(strips)] for j in range(2)]
-    halved = r.twos.at[role, pl.ds(strips * core, strips)]
-    send(c_half, halved, halved, partner)
-
-    def send_mate(i):
-        piece = r.twos.at[role, strips * core + i]
-        send(c_mate[i], piece, piece, mate)
-
-    send_mate(0)
 
     def combine(real, imag, axis):
         n = real.shape[axis] // 2
@@ -258,8 +211,56 @@
             )
         return carry
 
-    lax.fori_loop(0, blocks, load_of, 0)
-    own_given.wait()
+    lax.fori_loop(0, blocks, spread_of, 0)
+    lax.fori_loop(0, blocks // 2, load_of, 0)
+
+    def split_pair(slot):
+        def step_of(step, carry):
+            at = pl.ds(pl.multiple_of(step * STRIP, STRIP), STRIP)
+            for part in range(2):
+                r.pair_high[slot, part, at, :], r.pair_low[slot, part, at, :] = halves(
+                    r.pair[slot, part, at, :]
+                )
+            return carry
+
+        lax.fori_loop(0, size // STRIP, step_of, 0)
+
+    own_transfer.wait()
+    split_pair(core)
+    receive(c_transfer, r.pair.at[1 - core])
+    split_pair(1 - core)
+    first = (r.pair_high.at[0], r.pair_low.at[0])
+    second = (r.pair_high.at[1], r.pair_low.at[1])
+
+    def merged_rows(left, at, right):
+        rows_high = jnp.concatenate([left[0][0, at, :], left[0][1, at, :]], axis=0)
+        rows_low = jnp.concatenate([left[1][0, at, :], left[1][1, at, :]], axis=0)
+        out = [dot3((rows_high, rows_low), (right[0][part], right[1][part])) for part in range(2)]
+        return out[0][:STRIP] - out[1][STRIP:], out[0][STRIP:] + out[1][:STRIP]
+
+    half = size // 2
+    strips = half // STRIP
+
+    def merge_two(step, carry):
+        at = pl.ds(pl.multiple_of(core * half + step * STRIP, STRIP), STRIP)
+        merged = merged_rows(second, at, first)
+        for part in range(2):
+            r.twos[role, strips * core + step, part] = merged[part]
+        return carry
+
+    lax.fori_loop(0, half // STRIP, merge_two, 0)
+    c_half = channel()
+    c_mate = channel()
+    c_aside, c_pass = [[channel() for i in range(2)] for j in range(2)]
+    odd = x % 2
+    direct, indirect = strips * core + odd, strips * core + 1 - odd
+    halved = r.twos.at[role, pl.ds(strips * core, strips)]
+    send(c_half, halved, halved, partner)
+
+    piece = r.twos.at[role, direct]
+    send(c_mate, piece, piece, mate)
+
+    lax.fori_loop(blocks // 2, blocks, load_of, 0)
     given = jnp.concatenate([r.given[0], r.given[1]], axis=1)
     rest = (jnp.where(sub == 0, given, jnp.zeros_like(given)) - r.total[...]).T
     rest = rest.reshape(2, shots // 8, 8, size)
@@ -291,8 +292,13 @@
 
     r.forward_sum[...] = side_sum(0, other_sub)
     send(c_z, r.forward_sum, r.from_z, opposite)
-    for i in range(1, strips):
-        send_mate(i)
+
+    piece = r.twos.at[1 - role, direct]
+    receive(c_mate, piece)
+    for part in range(2):
+        aside = r.twos.at[1 - role, direct, part]
+        send(c_aside[part], aside, aside, beside[2 * part])
+    send(c_pass[0], piece, piece, partner)
     own_sum = side_sum(1, sub)
 
     receive(c_half, r.twos.at[role, pl.ds(strips * (1 - core), strips)])
@@ -354,12 +360,12 @@
             late_copy.start()
             early_copy.start()
 
-    for i in range(strips):
-        piece = r.twos.at[1 - role, strips * core + i]
-        receive(c_mate[i], piece)
-        send(c_pass[i], piece, piece, partner)
-    for i in range(strips):
-        receive(c_pass[i], r.twos.at[1 - role, strips * (1 - core) + i])
+    for part in range(2):
+        receive(c_aside[part], r.twos.at[1 - role, indirect, part])
+    piece = r.twos.at[1 - role, indirect]
+    send(c_pass[1], piece, piece, partner)
+    for i in range(2):
+        receive(c_pass[i], r.twos.at[1 - role, strips * (1 - core) + (odd if i == 0 else 1 - odd)])
     split_two(1 - role)
 
     @pl.when(jnp.logical_and(duo > 1, jnp.logical_or(late, upper == 0)))
@@ -610,8 +616,8 @@
     vmem = pltpu.VMEM
     inputs = {
         "rows": separator_rows[0],
+        "given": rhs_separator[0],
         "rhs_hbm": rhs_interior[0],
-        "separator_hbm": rhs_separator[0],
         "inverse_hbm": inverse_blocks[0],
         "coupling_hbm": coupling[0],
         "schur_hbm": separator_inverse[0],
@@ -639,7 +645,6 @@
         "known_low": vmem((m, 2 * shots), BF16),
         "weighted_high": vmem((size, 2 * shots), BF16),
         "weighted_low": vmem((size, 2 * shots), BF16),
-        "given": vmem((2, size, shots), F32),
         "total": vmem((size, 2 * shots), F32),
         "load": vmem((8, 32, size), F32),
         "from_x": vmem((2, 3, 32, size), F32),
@@ -681,7 +686,7 @@
         "found_low": vmem((2 * shots, size), BF16),
         "send_sem": pltpu.SemaphoreType.DMA((CHANNELS,)),
         "recv_sem": pltpu.SemaphoreType.DMA((CHANNELS,)),
-        "here_sem": pltpu.SemaphoreType.DMA((3,)),
+        "here_sem": pltpu.SemaphoreType.DMA((2,)),
         "block_sem": pltpu.SemaphoreType.DMA((3, nb)),
     }
     names = list(inputs) + list(outputs) + list(scratch)
@@ -692,12 +697,12 @@
     interior, separator = pl.pallas_call(
         sweep_kernel,
         out_shape=tuple(outputs.values()),
-        in_specs=[pl.BlockSpec(memory_space=pltpu.VMEM)]
-        + [pl.BlockSpec(memory_space=pltpu.HBM)] * (len(inputs) - 1),
+        in_specs=[pl.BlockSpec(memory_space=pltpu.VMEM)] * 2
+        + [pl.BlockSpec(memory_space=pltpu.HBM)] * (len(inputs) - 2),
         out_specs=(pl.BlockSpec(memory_space=pltpu.VMEM),) * 2,
         scratch_shapes=list(scratch.values()),
         compiler_params=pltpu.CompilerParams(
-            collective_id=0, has_side_effects=True, vmem_limit_bytes=61 << 20
+            collective_id=0, has_side_effects=True, vmem_limit_bytes=51 << 20
         ),
     )(*inputs.values())
     return (interior[None], separator[None])

time: 114 us -> 108 us (0.947)
  Pallas kernels: 109 us -> 103 us
    pallas_call x1, Pallas kernels: 109 us -> 103 us  [body(): pl.pallas_call(sweep_kernel, out_shape=tuple(outputs.values()), in_specs=...]
    unnamed x4 -> x6, local copies, waits for them, and re-layouts: 3.12 us -> 3.5 us
where the time goes in v5:
time: 108 us; the launch traced here: 107 us
  Pallas kernels  103 us (95%)
  local copies, waits for them, and re-layouts  3.5 us (3%)
    pallas_call x1, Pallas kernels, body(): pl.pallas_call(sweep_kernel, out_shape=tuple(outputs.values()), in_specs=...  103 us
    unnamed x6, local copies, waits for them, and re-layouts  3.5 us

profile of v5, /device:TPU:1, one launch (start us, length us, event | category | flops | bytes accessed | tf_op | source)
XLA Modules:
  0.0 107.5 jit_solution(9769207538486643170)
XLA Ops:
  0.6 0.0 copy-start
  0.6 1.0 copy-done
  1.7 0.0 copy-start.1
  1.7 0.7 copy-done.1
  2.4 103.3 %shard_map.86 = (f32[4,2,256,128]{3,2,1,0:T(8,128)S(1)}, f32[2,512,128]{2,1,0:T(8,128)S(1)}) custom-call(s32[4,512]{1,0:T(4,128)S(1)} %bitcast.12, f32[2,512,128]{2,1,0:T(8,128)S(1)} %bitcast.10, f32[4,2,256,128]{3,2,1,0:T(8,128)} %bitcast.17, f32[4,2,256,256]{3,2,1,0:T(8,128)} %bitcast.14, f32[4,2,512,256]{3,2,1,0:T(8,128)} %bitcast.13, ...), custom_call_target="tpu_custom_call" | custom-call | tf_op jit(solution)/shard_map/pallas_call | solution.py:697
  105.7 1.0 copy.11
  106.7 0.8 copy.12
Async XLA Ops:
  0.6 1.0 copy-start
  1.7 0.7 copy-start.1

commit v6 on v5

--- a/solution.py
+++ b/solution.py
@@ -13,6 +13,7 @@
 NN = (((1,), (0,)), ((), ()))
 NT = (((1,), (1,)), ((), ()))
 STRIP = 128
+WIDE = 256
 
 
 def halves(value):
@@ -59,6 +60,9 @@
     has_row_after, has_row_before = row < rows - 1, row > 0
     leads = jnp.logical_and(early, upper == 0)
     helps = jnp.logical_and(early, upper == 1)
+    enters = jnp.logical_and(late, upper == 0)
+    ends = jnp.logical_and(late, upper == 1)
+    node = jnp.logical_or(enters, helps)
     blocks, _, size, m = r.coupling_hbm.shape
     shots = r.rhs_hbm.shape[-1]
 
@@ -68,8 +72,11 @@
     across = (other_core, other_sub)
     mate = (slab + 2 - 4 * role, sub)
     beside = [(slab, ((x + d) % 4) * 2 + far) for d in (1, 2, 3)]
-    next_late, next_early = ((slab + 4) % slabs, sub), ((slab + 2) % slabs, sub)
-    last_early, last_late = ((slab + slabs - 4) % slabs, sub), ((slab + slabs - 2) % slabs, sub)
+    def chip_at(offset):
+        return ((slab + slabs + offset) % slabs, sub)
+
+    critical, other = chip_at(2 + 4 * upper), chip_at(4)
+    last_early, last_late = chip_at(-4), chip_at(-2)
     next_lead, last_lead = ((slab + 8) % slabs, sub), ((slab + slabs - 8) % slabs, sub)
 
     count = [0]
@@ -131,38 +138,31 @@
     for device in [partner, opposite, across, mate] + beside:
         greet(device)
 
-    @pl.when(has_after)
-    def _():
-        greet(next_late)
-
-        @pl.when(late)
-        def _():
-            greet(next_early)
-
-    @pl.when(has_before)
-    def _():
-        greet(last_early)
-
-        @pl.when(early)
-        def _():
-            greet(last_late)
-
-    @pl.when(jnp.logical_and(leads, has_row_after))
-    def _():
-        greet(next_lead)
-
-    @pl.when(jnp.logical_and(leads, has_row_before))
-    def _():
-        greet(last_lead)
+    for who, always, before_too, after_too in (
+        (leads, (4,), (-4, -2, -8), (8,)),
+        (enters, (2, 4), (-6,), ()),
+        (helps, (-2, -4), (), (4, 6)),
+        (ends, (-4,), (), (2,)),
+    ):
+        for when, offsets in (
+            (who, always),
+            (jnp.logical_and(who, has_row_before), before_too),
+            (jnp.logical_and(who, has_row_after), after_too),
+        ):
+            if offsets:
+
+                @pl.when(when)
+                def _(offsets=offsets):
+                    for offset in offsets:
+                        greet(chip_at(offset))
 
     pl.semaphore_wait(
         barrier,
         7
-        + after
-        + before
-        + role * after
-        + (1 - role) * before
-        + (1 - role) * (1 - upper) * (row_after + row_before),
+        + (1 - role) * (1 - upper) * (1 + 3 * row_before + row_after)
+        + role * (1 - upper) * (2 + row_before)
+        + (1 - role) * upper * (2 + 2 * row_after)
+        + role * upper * (1 + row_after),
     )
 
     c_transfer = channel()
@@ -191,19 +191,19 @@
                 out.append(dot3(left, right))
             return combine(out[0], out[1], 1)
 
-        for i in range(m // STRIP):
-            at = slice(i * STRIP, (i + 1) * STRIP)
+        for i in range(m // WIDE):
+            at = slice(i * WIDE, (i + 1) * WIDE)
             right = (r.rhs_high[...], r.rhs_low[...])
             value = strip(at, r.inverse, r.inverse_high, r.inverse_low, right)
             r.eliminated[b, at] = value
             r.known_high[at], r.known_low[at] = halves(value)
-        for i in range(size // STRIP):
-            at = slice(i * STRIP, (i + 1) * STRIP)
+        for i in range(size // WIDE):
+            at = slice(i * WIDE, (i + 1) * WIDE)
             right = (r.known_high[...], r.known_low[...])
             value = strip(at, r.coupling, r.coupling_high, r.coupling_low, right)
             r.weighted_high[at], r.weighted_low[at] = halves(value)
-        for i in range(size // STRIP):
-            at = slice(i * STRIP, (i + 1) * STRIP)
+        for i in range(size // WIDE):
+            at = slice(i * WIDE, (i + 1) * WIDE)
             spread = r.spread[b, at]
             r.total[at] += dot(
                 jnp.concatenate([spread, spread], axis=1),
@@ -269,7 +269,7 @@
     c_x = [[channel() for d in range(3)] for which in range(2)]
     c_z = channel()
     for which in range(2):
-        for d in (1, 2, 3):
+        for d in (2, 1, 3):
             group = 2 * ((x + d) % 4) + (1 - far if which == 0 else far)
             send(
                 c_x[which][d - 1], r.load.at[group], r.from_x.at[which, d - 1], beside[d - 1]
@@ -340,25 +340,26 @@
     receive(c_swap, r.local.at[1 - core])
     start = r.local[1] - times(r.local[0], second, NT)
     c_start = channel()
-    start_copy = send(c_start, r.start, r.start_in, mate, early)
+    gives_start = jnp.logical_or(early, upper == 1)
+    start_copy = send(c_start, r.start, r.start_in, mate, gives_start)
     r.start[...] = start
-    pl.when(early)(start_copy.start)
-
-    c_late, c_early = channel(), channel()
-    goes_on = jnp.logical_and(late, has_after)
-    late_copy = send(c_late, r.ahead_out, r.ahead_in, next_late, goes_on)
-    early_copy = send(c_early, r.ahead_out, r.ahead_in, next_early, goes_on)
-
-    @pl.when(late)
+    pl.when(gives_start)(start_copy.start)
+
+    c_node, c_other = channel(), channel()
+    goes_on = jnp.logical_and(node, has_after)
+    node_copy = send(c_node, r.ahead_out, r.ahead_in, critical, goes_on)
+    other_copy = send(c_other, r.ahead_out, r.ahead_in, other, goes_on)
+
+    @pl.when(enters)
     def _():
         receive(c_start, r.start_in)
-        r.start[...] += times(r.start_in[...], two_late, NT)
+        r.node_start[...] = r.start[...] + times(r.start_in[...], two_late, NT)
 
         @pl.when(jnp.logical_not(has_before))
         def _():
-            r.ahead_out[...] = r.start[...]
-            late_copy.start()
-            early_copy.start()
+            r.ahead_out[...] = r.node_start[...]
+            node_copy.start()
+            other_copy.start()
 
     for part in range(2):
         receive(c_aside[part], r.twos.at[1 - role, indirect, part])
@@ -368,25 +369,12 @@
         receive(c_pass[i], r.twos.at[1 - role, strips * (1 - core) + (odd if i == 0 else 1 - odd)])
     split_two(1 - role)
 
-    @pl.when(jnp.logical_and(duo > 1, jnp.logical_or(late, upper == 0)))
-    def _():
-        def merge_four(step, carry):
-            at = pl.ds(pl.multiple_of(step * STRIP, STRIP), STRIP)
-            merged = merged_rows(two_late, at, two_early)
-
-            @pl.when(early)
-            def _():
-                for part in range(2):
-                    r.four_high[part, at, :], r.four_low[part, at, :] = halves(merged[part])
-
-            @pl.when(late)
-            def _():
-                for part in range(2):
-                    r.four_high[part, :, at], r.four_low[part, :, at] = halves(merged[part].T)
-
-            return carry
-
-        lax.fori_loop(0, size // STRIP, merge_four, 0)
+    pl.when(ends)(lambda: receive(c_start, r.start_in))
+
+    @pl.when(helps)
+    def _():
+        receive(c_start, r.start_in)
+        r.node_start[...] = r.start_in[...] + times(r.start[...], two_late, NT)
 
     gives = jnp.logical_and(helps, has_row_after)
     takes = jnp.logical_and(leads, has_row_after)
@@ -394,17 +382,33 @@
     half_four = pl.ds(strips * core, strips)
     four_copy = send(c_four, r.four_out, r.four_in.at[half_four], last_early, gives)
 
-    @pl.when(gives)
-    def _():
-        def merge_half(step, carry):
-            at = pl.ds(pl.multiple_of(core * half + step * STRIP, STRIP), STRIP)
+    @pl.when(jnp.logical_or(gives, jnp.logical_and(upper == 0, duo > 1)))
+    def _():
+        def merge_four(step, carry):
+            at = pl.ds(pl.multiple_of(step * STRIP, STRIP), STRIP)
             merged = merged_rows(two_late, at, two_early)
-            for part in range(2):
-                r.four_out[step, part] = merged[part]
+
+            @pl.when(leads)
+            def _():
+                for part in range(2):
+                    r.four_high[part, at, :], r.four_low[part, at, :] = halves(merged[part])
+
+            @pl.when(node)
+            def _():
+                for part in range(2):
+                    r.four_high[part, :, at], r.four_low[part, :, at] = halves(merged[part].T)
+
+            @pl.when(step // strips == core)
+            def _():
+                for part in range(2):
+                    r.four_out[step % strips, part] = merged[part]
+
             return carry
 
-        lax.fori_loop(0, strips, merge_half, 0)
-        four_copy.start()
+        whole = (duo + duos - 3) // (duos - 1)
+        low = (1 - whole) * strips * core
+        lax.fori_loop(low, low + strips * (1 + whole), merge_four, 0)
+        pl.when(gives)(four_copy.start)
 
     def weights_of(b, carry):
         spread = r.spread[b]
@@ -439,37 +443,41 @@
     def _():
         lax.fori_loop(0, blocks, weights_of, 0)
 
+    @pl.when(jnp.logical_and(node, has_before))
+    def _():
+        receive(c_node, r.ahead_in)
+
+        @pl.when(jnp.logical_and(duo > 1, has_after))
+        def _():
+            r.ahead_out[...] = r.node_start[...] + times(r.ahead_in[...], four, NN)
+
+        @pl.when(duo == 1)
+        def _():
+            r.ahead_out[...] = r.node_start[...] + times(
+                times(r.ahead_in[...], two_early, NT), two_late, NT
+            )
+
+        @pl.when(has_after)
+        def _():
+            node_copy.start()
+            other_copy.start()
+
+    @pl.when(ends)
+    def _():
+        receive(c_other, r.ahead_in)
+
+    @pl.when(jnp.logical_and(leads, has_before))
+    def _():
+        receive(c_other, r.ahead_in)
+
+    r.enter[...] = r.ahead_in[...]
+
     @pl.when(late)
     def _():
-        @pl.when(has_before)
-        def _():
-            receive(c_late, r.ahead_in)
-
-            @pl.when(duo > 1)
-            def _():
-                r.ahead_out[...] = r.start[...] + times(r.ahead_in[...], four, NN)
-
-            @pl.when(duo == 1)
-            def _():
-                r.ahead_out[...] = r.start[...] + times(
-                    times(r.ahead_in[...], two_early, NT), two_late, NT
-                )
-
-            @pl.when(has_after)
-            def _():
-                late_copy.start()
-                early_copy.start()
-
-        r.trace[1] = r.ahead_out[...]
-        inner = r.start_in[...] + times(r.ahead_in[...], two_early, NT)
-        r.trace[0] = r.local[0] - times(inner, first, NT)
-
-    @pl.when(early)
-    def _():
-        pl.when(has_before)(lambda: receive(c_early, r.ahead_in))
-        r.trace[0] = r.local[0] - times(r.ahead_in[...], first, NT)
-        r.trace[1] = r.local[1] - times(r.trace[0], second, NT)
-
+        r.enter[...] = r.start_in[...] + times(r.ahead_in[...], two_early, NT)
+
+    r.trace[0] = r.local[0] - times(r.enter[...], first, NT)
+    r.trace[1] = r.local[1] - times(r.trace[0], second, NT)
     queued = times(r.trace[0] - times(r.trace[1], second, NN), first, NN)
     r.queued[...] = queued
     c_queued = channel()
@@ -541,12 +549,12 @@
 
         r.carried[...] = r.queued_in[...] + times(r.lower[...], two_late, NN)
 
-    @pl.when(jnp.logical_and(late, upper == 1))
+    @pl.when(ends)
     def _():
         pl.when(has_row_after)(lambda: receive(c_back_late, r.back_in))
         r.carried[...] = r.back_in[...]
 
-    @pl.when(jnp.logical_and(late, upper == 0))
+    @pl.when(enters)
     def _():
         receive(c_lower, r.lower_in)
         r.carried[...] = r.lower_in[...]
@@ -562,11 +570,11 @@
     send(c_across, r.found.at[1 - core], place, across)
     r.gathered[sub, core] = r.found[core]
     receive(c_chip, r.gathered.at[sub, 1 - core])
-    for d in (1, 2, 3):
+    for d in (2, 1, 3):
         send(c_side[0][d - 1], r.gathered.at[sub], r.gathered.at[sub], beside[d - 1])
     receive(c_far, r.gathered.at[other_sub, core])
     receive(c_across, r.gathered.at[other_sub, 1 - core])
-    for d in (1, 2, 3):
+    for d in (2, 1, 3):
         send(c_side[1][d - 1], r.gathered.at[other_sub], r.gathered.at[other_sub], beside[d - 1])
     for which in range(2):
         for d in (1, 2, 3):
@@ -672,6 +680,8 @@
         "local": vmem((2, 16, size), F32),
         "start": vmem((16, size), F32),
         "start_in": vmem((16, size), F32),
+        "node_start": vmem((16, size), F32),
+        "enter": vmem((16, size), F32),
         "ahead_in": vmem((16, size), F32),
         "ahead_out": vmem((16, size), F32),
         "trace": vmem((2, 16, size), F32),

time: 108 us -> 128 us (1.19); the launches traced: 107 us -> 126 us
  Pallas kernels: 103 us -> 122 us
    pallas_call x1, Pallas kernels: 103 us -> 122 us  [body(): pl.pallas_call(sweep_kernel, out_shape=tuple(outputs.values()), in_specs=...]
where the time goes in v6:
time: 128 us; the launch traced here: 126 us
  Pallas kernels  122 us (95%)
  local copies, waits for them, and re-layouts  3.5 us (3%)
    pallas_call x1, Pallas kernels, body(): pl.pallas_call(sweep_kernel, out_shape=tuple(outputs.values()), in_specs=...  122 us
    unnamed x6, local copies, waits for them, and re-layouts  3.5 us

profile of v6, /device:TPU:1, one launch (start us, length us, event | category | flops | bytes accessed | tf_op | source)
XLA Modules:
  0.0 126.2 jit_solution(17607305471225760752)
XLA Ops:
  0.6 0.0 copy-start
  0.6 1.0 copy-done
  1.7 0.0 copy-start.1
  1.7 0.7 copy-done.1
  2.4 122.0 %shard_map.86 = (f32[4,2,256,128]{3,2,1,0:T(8,128)S(1)}, f32[2,512,128]{2,1,0:T(8,128)S(1)}) custom-call(s32[4,512]{1,0:T(4,128)S(1)} %bitcast.12, f32[2,512,128]{2,1,0:T(8,128)S(1)} %bitcast.10, f32[4,2,256,128]{3,2,1,0:T(8,128)} %bitcast.17, f32[4,2,256,256]{3,2,1,0:T(8,128)} %bitcast.14, f32[4,2,512,256]{3,2,1,0:T(8,128)} %bitcast.13, ...), custom_call_target="tpu_custom_call" | custom-call | tf_op jit(solution)/shard_map/pallas_call | solution.py:707
  124.4 1.0 copy.11
  125.4 0.8 copy.12
Async XLA Ops:
  0.6 1.0 copy-start
  1.7 0.7 copy-start.1

commit v7 on v6

--- a/solution.py
+++ b/solution.py
@@ -378,9 +378,14 @@
 
     gives = jnp.logical_and(helps, has_row_after)
     takes = jnp.logical_and(leads, has_row_after)
-    c_four, c_four_pass = channel(), channel()
+    c_four, c_four_pass = [channel() for i in range(strips)], channel()
     half_four = pl.ds(strips * core, strips)
-    four_copy = send(c_four, r.four_out, r.four_in.at[half_four], last_early, gives)
+    four_copies = [
+        send(c_four[i], r.four_out.at[i], r.four_in.at[strips * core + i], last_early, gives)
+        for i in range(strips)
+    ]
+    soon = jnp.logical_and(helps, row == rows - 2)
+    not_soon = jnp.logical_and(helps, row < rows - 2)
 
     @pl.when(jnp.logical_or(gives, jnp.logical_and(upper == 0, duo > 1)))
     def _():
@@ -408,7 +413,7 @@
         whole = (duo + duos - 3) // (duos - 1)
         low = (1 - whole) * strips * core
         lax.fori_loop(low, low + strips * (1 + whole), merge_four, 0)
-        pl.when(gives)(four_copy.start)
+        pl.when(soon)(four_copies[0].start)
 
     def weights_of(b, carry):
         spread = r.spread[b]
@@ -462,6 +467,13 @@
             node_copy.start()
             other_copy.start()
 
+    pl.when(not_soon)(four_copies[0].start)
+
+    @pl.when(gives)
+    def _():
+        for copy in four_copies[1:]:
+            copy.start()
+
     @pl.when(ends)
     def _():
         receive(c_other, r.ahead_in)
@@ -515,7 +527,8 @@
     def _():
         @pl.when(has_row_after)
         def _():
-            receive(c_four, r.four_in.at[half_four])
+            for i in range(strips):
+                receive(c_four[i], r.four_in.at[strips * core + i])
             pass_copy.start()
             receive(c_four_pass, r.four_in.at[pl.ds(strips * (1 - core), strips)])
 
@@ -607,7 +620,7 @@
             pl.when(when)(copy.wait_send)
 
 
-CHANNELS = 40
+CHANNELS = 44
 
 
 def body(

time: 128 us -> 107 us (0.84)
  Pallas kernels: 122 us -> 102 us
    pallas_call x1, Pallas kernels: 122 us -> 102 us  [body(): pl.pallas_call(sweep_kernel, out_shape=tuple(outputs.values()), in_specs=...]
where the time goes in v7:
time: 107 us; the launch traced here: 106 us
  Pallas kernels  102 us (95%)
  local copies, waits for them, and re-layouts  3.5 us (3%)
    pallas_call x1, Pallas kernels, body(): pl.pallas_call(sweep_kernel, out_shape=tuple(outputs.values()), in_specs=...  102 us
    unnamed x6, local copies, waits for them, and re-layouts  3.5 us

profile of v7, /device:TPU:1, one launch (start us, length us, event | category | flops | bytes accessed | tf_op | source)
XLA Modules:
  0.0 106.3 jit_solution(5352959884987519464)
XLA Ops:
  0.6 0.0 copy-start
  0.6 1.0 copy-done
  1.7 0.0 copy-start.1
  1.7 0.7 copy-done.1
  2.4 102.2 %shard_map.86 = (f32[4,2,256,128]{3,2,1,0:T(8,128)S(1)}, f32[2,512,128]{2,1,0:T(8,128)S(1)}) custom-call(s32[4,512]{1,0:T(4,128)S(1)} %bitcast.12, f32[2,512,128]{2,1,0:T(8,128)S(1)} %bitcast.10, f32[4,2,256,128]{3,2,1,0:T(8,128)} %bitcast.17, f32[4,2,256,256]{3,2,1,0:T(8,128)} %bitcast.14, f32[4,2,512,256]{3,2,1,0:T(8,128)} %bitcast.13, ...), custom_call_target="tpu_custom_call" | custom-call | tf_op jit(solution)/shard_map/pallas_call | solution.py:720
  104.5 1.0 copy.11
  105.5 0.8 copy.12
Async XLA Ops:
  0.6 1.0 copy-start
  1.7 0.7 copy-start.1

commit v8 on v6

--- a/solution.py
+++ b/solution.py
@@ -378,11 +378,22 @@
 
     gives = jnp.logical_and(helps, has_row_after)
     takes = jnp.logical_and(leads, has_row_after)
-    c_four, c_four_pass = channel(), channel()
-    half_four = pl.ds(strips * core, strips)
-    four_copy = send(c_four, r.four_out, r.four_in.at[half_four], last_early, gives)
-
-    @pl.when(jnp.logical_or(gives, jnp.logical_and(upper == 0, duo > 1)))
+    c_four = channel()
+    c_four_aside, c_four_pass = [[channel() for i in range(2)] for j in range(2)]
+    four_copy = send(c_four, r.four_out, r.four_in.at[direct], last_early, gives)
+    soon = jnp.logical_and(helps, row == rows - 2)
+    not_soon = jnp.logical_and(helps, row < rows - 2)
+
+    def give():
+        at = pl.ds(pl.multiple_of(direct * STRIP, STRIP), STRIP)
+        merged = merged_rows(two_late, at, two_early)
+        for part in range(2):
+            r.four_out[part] = merged[part]
+        four_copy.start()
+
+    pl.when(soon)(give)
+
+    @pl.when(jnp.logical_and(duo > 1, jnp.logical_or(gives, upper == 0)))
     def _():
         def merge_four(step, carry):
             at = pl.ds(pl.multiple_of(step * STRIP, STRIP), STRIP)
@@ -398,17 +409,9 @@
                 for part in range(2):
                     r.four_high[part, :, at], r.four_low[part, :, at] = halves(merged[part].T)
 
-            @pl.when(step // strips == core)
-            def _():
-                for part in range(2):
-                    r.four_out[step % strips, part] = merged[part]
-
             return carry
 
-        whole = (duo + duos - 3) // (duos - 1)
-        low = (1 - whole) * strips * core
-        lax.fori_loop(low, low + strips * (1 + whole), merge_four, 0)
-        pl.when(gives)(four_copy.start)
+        lax.fori_loop(0, size // STRIP, merge_four, 0)
 
     def weights_of(b, carry):
         spread = r.spread[b]
@@ -462,6 +465,8 @@
             node_copy.start()
             other_copy.start()
 
+    pl.when(not_soon)(give)
+
     @pl.when(ends)
     def _():
         receive(c_other, r.ahead_in)
@@ -495,9 +500,13 @@
     back_lead = send(c_lead, r.back_out, r.back_in, last_lead, goes_back)
     back_help = send(c_help, r.back_out, r.back_in, last_early, goes_back)
     back_late = send(c_back_late, r.back_out, r.back_in, last_late, goes_back)
-    pass_copy = send(
-        c_four_pass, r.four_in.at[half_four], r.four_in.at[half_four], partner, takes
-    )
+    piece = r.four_in.at[direct]
+    take_copies = [
+        send(c_four_aside[part], piece.at[part], piece.at[part], beside[2 * part], takes)
+        for part in range(2)
+    ] + [send(c_four_pass[0], piece, piece, partner, takes)]
+    piece = r.four_in.at[indirect]
+    pass_copy = send(c_four_pass[1], piece, piece, partner, takes)
     top = (r.top_high, r.top_low)
 
     @pl.when(early)
@@ -515,9 +524,17 @@
     def _():
         @pl.when(has_row_after)
         def _():
-            receive(c_four, r.four_in.at[half_four])
+            receive(c_four, r.four_in.at[direct])
+            for copy in take_copies:
+                copy.start()
+            for part in range(2):
+                receive(c_four_aside[part], r.four_in.at[indirect, part])
             pass_copy.start()
-            receive(c_four_pass, r.four_in.at[pl.ds(strips * (1 - core), strips)])
+            for i in range(2):
+                receive(
+                    c_four_pass[i],
+                    r.four_in.at[strips * (1 - core) + (odd if i == 0 else 1 - odd)],
+                )
 
             def split_top(step, carry):
                 to = pl.ds(pl.multiple_of(step * STRIP, STRIP), STRIP)
@@ -607,7 +624,7 @@
             pl.when(when)(copy.wait_send)
 
 
-CHANNELS = 40
+CHANNELS = 48
 
 
 def body(
@@ -669,7 +686,7 @@
         "two_low": vmem((2, 2, size, size), BF16),
         "four_high": vmem((2, size, size), BF16),
         "four_low": vmem((2, size, size), BF16),
-        "four_out": vmem((size // STRIP // 2, 2, STRIP, size), F32),
+        "four_out": vmem((2, STRIP, size), F32),
         "four_in": vmem((size // STRIP, 2, STRIP, size), F32),
         "top_high": vmem((2, size, size), BF16),
         "top_low": vmem((2, size, size), BF16),

time: 128 us -> 106 us (0.83)
  Pallas kernels: 122 us -> 101 us
    pallas_call x1, Pallas kernels: 122 us -> 101 us  [body(): pl.pallas_call(sweep_kernel, out_shape=tuple(outputs.values()), in_specs=...]
where the time goes in v8:
time: 106 us; the launch traced here: 105 us
  Pallas kernels  101 us (95%)
  local copies, waits for them, and re-layouts  3.5 us (3%)
    pallas_call x1, Pallas kernels, body(): pl.pallas_call(sweep_kernel, out_shape=tuple(outputs.values()), in_specs=...  101 us
    unnamed x6, local copies, waits for them, and re-layouts  3.5 us

profile of v8, /device:TPU:1, one launch (start us, length us, event | category | flops | bytes accessed | tf_op | source)
XLA Modules:
  0.0 105.0 jit_solution(17024355852221345694)
XLA Ops:
  0.6 0.0 copy-start
  0.6 1.0 copy-done
  1.7 0.0 copy-start.1
  1.7 0.7 copy-done.1
  2.4 100.8 %shard_map.86 = (f32[4,2,256,128]{3,2,1,0:T(8,128)S(1)}, f32[2,512,128]{2,1,0:T(8,128)S(1)}) custom-call(s32[4,512]{1,0:T(4,128)S(1)} %bitcast.12, f32[2,512,128]{2,1,0:T(8,128)S(1)} %bitcast.10, f32[4,2,256,128]{3,2,1,0:T(8,128)} %bitcast.17, f32[4,2,256,256]{3,2,1,0:T(8,128)} %bitcast.14, f32[4,2,512,256]{3,2,1,0:T(8,128)} %bitcast.13, ...), custom_call_target="tpu_custom_call" | custom-call | tf_op jit(solution)/shard_map/pallas_call | solution.py:724
  103.2 1.0 copy.11
  104.2 0.8 copy.12
Async XLA Ops:
  0.6 1.0 copy-start
  1.7 0.7 copy-start.1

commit v9 on v8

--- a/solution.py
+++ b/solution.py
@@ -156,6 +156,7 @@
                     for offset in offsets:
                         greet(chip_at(offset))
 
+    lax.fori_loop(0, blocks, spread_of, 0)
     pl.semaphore_wait(
         barrier,
         7
@@ -211,7 +212,6 @@
             )
         return carry
 
-    lax.fori_loop(0, blocks, spread_of, 0)
     lax.fori_loop(0, blocks // 2, load_of, 0)
 
     def split_pair(slot):
@@ -241,24 +241,23 @@
     half = size // 2
     strips = half // STRIP
 
-    def merge_two(step, carry):
-        at = pl.ds(pl.multiple_of(core * half + step * STRIP, STRIP), STRIP)
-        merged = merged_rows(second, at, first)
-        for part in range(2):
-            r.twos[role, strips * core + step, part] = merged[part]
-        return carry
-
-    lax.fori_loop(0, half // STRIP, merge_two, 0)
     c_half = channel()
     c_mate = channel()
     c_aside, c_pass = [[channel() for i in range(2)] for j in range(2)]
     odd = x % 2
     direct, indirect = strips * core + odd, strips * core + 1 - odd
+
+    def merge_two(strip):
+        merged = merged_rows(second, pl.ds(pl.multiple_of(strip * STRIP, STRIP), STRIP), first)
+        for part in range(2):
+            r.twos[role, strip, part] = merged[part]
+
+    merge_two(direct)
+    piece = r.twos.at[role, direct]
+    send(c_mate, piece, piece, mate)
+    merge_two(indirect)
     halved = r.twos.at[role, pl.ds(strips * core, strips)]
     send(c_half, halved, halved, partner)
-
-    piece = r.twos.at[role, direct]
-    send(c_mate, piece, piece, mate)
 
     lax.fori_loop(blocks // 2, blocks, load_of, 0)
     given = jnp.concatenate([r.given[0], r.given[1]], axis=1)
@@ -582,9 +581,9 @@
     c_chip, c_far, c_across = channel(), channel(), channel()
     c_side = [[channel() for d in range(3)] for which in range(2)]
     place = r.gathered.at[sub, core]
-    send(c_chip, r.found.at[1 - core], place, partner)
     send(c_far, r.found.at[core], place, opposite)
     send(c_across, r.found.at[1 - core], place, across)
+    send(c_chip, r.found.at[1 - core], place, partner)
     r.gathered[sub, core] = r.found[core]
     receive(c_chip, r.gathered.at[sub, 1 - core])
     for d in (2, 1, 3):

time: 106 us -> 105 us (level)
  Pallas kernels: 101 us -> 99.9 us
where the time goes in v9:
time: 105 us; the launch traced here: 104 us
  Pallas kernels  99.9 us (95%)
  local copies, waits for them, and re-layouts  3.5 us (3%)
    pallas_call x1, Pallas kernels, body(): pl.pallas_call(sweep_kernel, out_shape=tuple(outputs.values()), in_specs=...  99.9 us
    unnamed x6, local copies, waits for them, and re-layouts  3.5 us

profile of v9, /device:TPU:1, one launch (start us, length us, event | category | flops | bytes accessed | tf_op | source)
XLA Modules:
  0.0 104.0 jit_solution(17013603304729648735)
XLA Ops:
  0.6 0.0 copy-start
  0.6 1.0 copy-done
  1.7 0.0 copy-start.1
  1.7 0.7 copy-done.1
  2.4 99.9 %shard_map.86 = (f32[4,2,256,128]{3,2,1,0:T(8,128)S(1)}, f32[2,512,128]{2,1,0:T(8,128)S(1)}) custom-call(s32[4,512]{1,0:T(4,128)S(1)} %bitcast.12, f32[2,512,128]{2,1,0:T(8,128)S(1)} %bitcast.10, f32[4,2,256,128]{3,2,1,0:T(8,128)} %bitcast.17, f32[4,2,256,256]{3,2,1,0:T(8,128)} %bitcast.14, f32[4,2,512,256]{3,2,1,0:T(8,128)} %bitcast.13, ...), custom_call_target="tpu_custom_call" | custom-call | tf_op jit(solution)/shard_map/pallas_call | solution.py:723
  102.2 1.0 copy.11
  103.2 0.8 copy.12
Async XLA Ops:
  0.6 1.0 %copy-start = (f32[1,2,512,128]{3,2,1,0:T(8,128)S(1)}, f32[1,2,512,128]{3,2,1,0:T(8,128)}, u32[]{:S(2)}) copy-start(f32[1,2,512,128]{3,2,1,0:T(8,128)} %param.8) | copy-start | bytes 1572868
  1.7 0.7 copy-start.1

commit v10 on v9

--- a/solution.py
+++ b/solution.py
@@ -212,7 +212,7 @@
             )
         return carry
 
-    lax.fori_loop(0, blocks // 2, load_of, 0)
+    lax.fori_loop(0, blocks // 2, load_of, 0, unroll=True)
 
     def split_pair(slot):
         def step_of(step, carry):
@@ -259,7 +259,7 @@
     halved = r.twos.at[role, pl.ds(strips * core, strips)]
     send(c_half, halved, halved, partner)
 
-    lax.fori_loop(blocks // 2, blocks, load_of, 0)
+    lax.fori_loop(blocks // 2, blocks, load_of, 0, unroll=True)
     given = jnp.concatenate([r.given[0], r.given[1]], axis=1)
     rest = (jnp.where(sub == 0, given, jnp.zeros_like(given)) - r.total[...]).T
     rest = rest.reshape(2, shots // 8, 8, size)
@@ -614,7 +614,7 @@
         r.interior_out[b, 1] = turned[:, shots:]
         return carry
 
-    lax.fori_loop(0, blocks, interior_of, 0)
+    lax.fori_loop(0, blocks, interior_of, 0, unroll=True)
 
     for copy, when in unsent:
         if when is None:

time: 105 us -> 104 us (level)
  Pallas kernels: 99.9 us -> 98.6 us
    pallas_call x1, Pallas kernels: 99.9 us -> 98.6 us  [body(): pl.pallas_call(sweep_kernel, out_shape=tuple(outputs.values()), in_specs=...]
where the time goes in v10:
time: 104 us; the launch traced here: 103 us
  Pallas kernels  98.6 us (95%)
  local copies, waits for them, and re-layouts  3.5 us (3%)
    pallas_call x1, Pallas kernels, body(): pl.pallas_call(sweep_kernel, out_shape=tuple(outputs.values()), in_specs=...  98.6 us
    unnamed x6, local copies, waits for them, and re-layouts  3.5 us

profile of v10, /device:TPU:1, one launch (start us, length us, event | category | flops | bytes accessed | tf_op | source)
XLA Modules:
  0.0 102.8 jit_solution(12101042926828677546)
XLA Ops:
  0.6 0.0 copy-start
  0.6 1.0 %copy-done = f32[1,2,512,128]{3,2,1,0:T(8,128)S(1)} copy-done((f32[1,2,512,128]{3,2,1,0:T(8,128)S(1)}, f32[1,2,512,128]{3,2,1,0:T(8,128)}, u32[]{:S(2)}) %copy-start) | copy-done | bytes 524312
  1.7 0.0 copy-start.1
  1.7 0.7 copy-done.1
  2.4 98.6 %shard_map.86 = (f32[4,2,256,128]{3,2,1,0:T(8,128)S(1)}, f32[2,512,128]{2,1,0:T(8,128)S(1)}) custom-call(s32[4,512]{1,0:T(4,128)S(1)} %bitcast.12, f32[2,512,128]{2,1,0:T(8,128)S(1)} %bitcast.10, f32[4,2,256,128]{3,2,1,0:T(8,128)} %bitcast.17, f32[4,2,256,256]{3,2,1,0:T(8,128)} %bitcast.14, f32[4,2,512,256]{3,2,1,0:T(8,128)} %bitcast.13, ...), custom_call_target="tpu_custom_call" | custom-call | tf_op jit(solution)/shard_map/pallas_call | solution.py:723
  101.0 1.0 copy.11
  102.0 0.8 copy.12
Async XLA Ops:
  0.6 1.0 %copy-start = (f32[1,2,512,128]{3,2,1,0:T(8,128)S(1)}, f32[1,2,512,128]{3,2,1,0:T(8,128)}, u32[]{:S(2)}) copy-start(f32[1,2,512,128]{3,2,1,0:T(8,128)} %param.8) | copy-start | bytes 1572868
  1.7 0.7 copy-start.1
